TPU v7x, 32 devices: a whole 2x2x4 slice. The times are simulated.
32 devices in a mesh: row: 4 (over y, x), col: 8 (over z, core).
Axes of the slice: x: 2, y: 2, z: 4, core: 2. Of those that a mesh axis runs over, the one named last changes fastest.
Arguments:
- trailing: float32 [3072, 3072], P('row', 'col'), may hold values from -6 to 6, as said below
- v_panels: bfloat16 [3, 3072, 256], P(None, ('row', 'col')), may hold values from -6 to 6
Outputs:
- updated: float32 [3072, 3072], P('row', 'col')
- w_panels: float32 [3, 3072, 256], P(None, ('row', 'col'))
Inputs may be any that keep to these rules, and one draw needn't show every extreme that they name: trailing is symmetric: entry (i, j) equals entry (j, i).
All inputs are finite; a program needn't handle non-finite values.
Results may differ from a plain program's by a relative error of at most 0.0003.
Values may be sent and summed in bfloat16 or wider, within the bound.
A program may use at most 64 MiB of HBM per device.

v0:
```python
import functools
import math

import jax
import jax.numpy as jnp
from jax import lax
from jax.experimental import pallas as pl
from jax.experimental.pallas import tpu as pltpu
from jax.sharding import PartitionSpec as P

MESH = pl.DeviceIdType.MESH
SPLITS = 3
NT = (((1,), (1,)), ((), ()))
NN = (((1,), (0,)), ((), ()))


def dot(a, b, dims):
    return lax.dot_general(a, b, dims, preferred_element_type=jnp.float32)


def kernel(
    nrow, ncol, ratio, scaling,
    a_ref, v_ref, out_ref, w_ref,
    b_ref, vr, vt, part, got, wc, wr,
    v_send, v_recv, vt_send, vt_recv, vx_send, vx_recv,
    rs_send, rs_recv, wc_send, wc_recv, wr_send, wr_recv, local_sem,
):
    ticks, piece, depth = v_ref.shape
    rows_tile, cols_tile = a_ref.shape
    links = ncol // ratio
    r = lax.axis_index("row")
    c = lax.axis_index("col")
    q = c // ratio
    j = c % ratio
    half = 0.5 * scaling

    splits = rs_recv.shape[1]
    chunk = piece // splits

    def rows(at):
        return pl.ds(pl.multiple_of(at * piece, piece), piece)

    def some(at, s):
        return pl.ds(pl.multiple_of(at * piece + s * chunk, chunk), chunk)

    def remote(src, dst, send, recv, row, col):
        return pltpu.make_async_remote_copy(
            src_ref=src, dst_ref=dst, send_sem=send, recv_sem=recv,
            device_id=(row, col), device_id_type=MESH,
        )

    from_row, from_col = c // ratio, j * nrow + r
    to_row, to_col = c % nrow, r * ratio + c // nrow
    stays = jnp.logical_and(to_row == r, to_col == c)

    barrier = pltpu.get_barrier_semaphore()
    for i in range(1, nrow):
        pl.semaphore_signal(barrier, inc=1, device_id=((r + i) % nrow, c), device_id_type=MESH)
    for i in range(1, ncol):
        pl.semaphore_signal(barrier, inc=1, device_id=(r, (c + i) % ncol), device_id_type=MESH)

    @pl.when(jnp.logical_not(stays))
    def _():
        pl.semaphore_signal(barrier, inc=1, device_id=(from_row, from_col), device_id_type=MESH)
        pl.semaphore_signal(barrier, inc=1, device_id=(to_row, to_col), device_id_type=MESH)

    pl.semaphore_wait(barrier, nrow + ncol - 2 + jnp.where(stays, 0, 2))

    def v_out(t, i):
        return remote(
            v_ref.at[t], vr.at[t, rows(c)], v_send.at[t, i], v_recv.at[t, c],
            r, ((q + i) % links) * ratio + j,
        )

    def v_side(t, i, k):
        src_col = ((q + i) % links) * ratio + j
        src = v_ref.at[t] if i == 0 else vr.at[t, rows(src_col)]
        return remote(
            src, vr.at[t, rows(src_col)], vx_send.at[t, i, k - 1], v_recv.at[t, src_col],
            r, q * ratio + (j + k) % ratio,
        )

    def v_own(t):
        return pltpu.make_async_copy(v_ref.at[t], vr.at[t, rows(c)], v_recv.at[t, c])

    def v_in(t, col):
        return pltpu.make_async_copy(v_ref.at[t], vr.at[t, rows(col)], v_recv.at[t, col])

    def v_start(t):
        for i in range(1, links):
            v_out(t, i).start()
        for k in range(1, ratio):
            v_side(t, 0, k).start()
        v_own(t).start()

    vt_move = remote(v_ref, vt.at[:, rows(to_row)], vt_send, vt_recv, to_row, to_col)
    vt_in = pltpu.make_async_copy(v_ref, vt.at[:, rows(r)], vt_recv)

    v_start(0)

    @pl.when(stays)
    def _():
        vt_in.start()

    @pl.when(jnp.logical_not(stays))
    def _():
        vt_move.start()

    for t in range(1, ticks):
        v_start(t)

    b_ref[...] = a_ref[...].T

    def v_relay(t):
        for i in range(1, links):
            v_in(t, ((q + i) % links) * ratio + j).wait()
            for k in range(1, ratio):
                v_side(t, i, k).start()

    def v_finish(t):
        v_in(t, c).wait()
        for i in range(links):
            for k in range(1, ratio):
                v_in(t, ((q + i) % links) * ratio + (j + k) % ratio).wait()

    def rs_out(t, s, i):
        peer = (r + i) % nrow
        return remote(
            part.at[t, some(peer, s)], got.at[t, some(r, s)],
            rs_send.at[t, s, i], rs_recv.at[t, s, r], peer, c,
        )

    def rs_in(t, s, peer):
        return pltpu.make_async_copy(
            part.at[t, some(peer, s)], got.at[t, some(peer, s)], rs_recv.at[t, s, peer]
        )

    def wc_out(t, s, i):
        peer = (r + i) % nrow
        spot = wc.at[t, :, some(r, s)]
        return remote(spot, spot, wc_send.at[t, s, i], wc_recv.at[t, s, r], peer, c)

    def wc_in(t, s, peer):
        spot = wc.at[t, :, some(peer, s)]
        return pltpu.make_async_copy(spot, spot, wc_recv.at[t, s, peer])

    def vt_out(t, i):
        peer = (r + i) % nrow
        spot = vt.at[t, rows(r)]
        return remote(spot, spot, vx_send.at[t, links + i - 1, 0], vx_recv.at[t, r], peer, c)

    def vt_got(t, peer):
        spot = vt.at[t, rows(peer)]
        return pltpu.make_async_copy(spot, spot, vx_recv.at[t, peer])

    source = q == r
    up = jnp.logical_and(q >= r, q < links - 1)
    down = jnp.logical_and(q <= r, q > 0)

    def wr_spot(t, s, seat, peer):
        return wr.at[t, :, some(seat * nrow + peer, s)]

    def wr_out(t, s, i, way, first):
        peer = (r + i) % nrow
        spot = wr_spot(t, s, j, peer)
        src = wc.at[t, :, some(peer, s)] if first else spot
        if way == 0:
            col = c + ratio
        elif way == 1:
            col = c - ratio
        else:
            col = q * ratio + (j + way - 1) % ratio
        return remote(
            src, spot, wr_send.at[t, s, i, way], wr_recv.at[t, s, j * nrow + peer], r, col
        )

    def wr_in(t, s, seat, peer):
        spot = wr_spot(t, s, seat, peer)
        return pltpu.make_async_copy(spot, spot, wr_recv.at[t, s, seat * nrow + peer])

    def wr_keep(t, s, i):
        peer = (r + i) % nrow
        return pltpu.make_async_copy(
            wc.at[t, :, some(peer, s)], wr_spot(t, s, j, peer), local_sem.at[t, s, i]
        )

    def wr_ways(t, s, i, first, act):
        @pl.when(up)
        def _():
            act(wr_out(t, s, i, 0, first))

        @pl.when(down)
        def _():
            act(wr_out(t, s, i, 1, first))

        for k in range(1, ratio):
            act(wr_out(t, s, i, 1 + k, first))

    def start(copy):
        copy.start()

    def wait_send(copy):
        copy.wait_send()

    def seat_rows(seat):
        return pl.ds(pl.multiple_of(seat * cols_tile, cols_tile), cols_tile)

    def update_v(t):
        out_ref[...] = (out_ref if t else a_ref)[...] - half * (
            dot(vr[t], wc[t, 0], NT) + dot(vr[t], wc[t, 1], NT)
        )

    def update_w(t, seat):
        at = seat_rows(seat)
        out_ref[at] -= half * (dot(wr[t, 0, at], vt[t], NT) + dot(wr[t, 1, at], vt[t], NT))

    def turn_w(t, seat):
        at = seat_rows(seat)
        b_ref[:, at] -= half * (dot(vt[t], wr[t, 0, at], NT) + dot(vt[t], wr[t, 1, at], NT))

    for t in range(ticks):
        last = t == ticks - 1
        if t == 0:
            v_relay(0)
            v_finish(0)
        high = b_ref[...].astype(jnp.bfloat16)
        low = (b_ref[...] - high.astype(jnp.float32)).astype(jnp.bfloat16)
        part[t] = dot(high, vr[t], NN) + dot(low, vr[t], NN)
        for s in range(splits):
            for i in range(1, nrow):
                rs_out(t, s, i).start()
        for s in range(splits):
            total = part[t, some(r, s)]
            for i in range(1, nrow):
                peer = (r + i) % nrow
                rs_in(t, s, peer).wait()
                total = total + got[t, some(peer, s)]
            total = total * scaling
            head = total.astype(jnp.bfloat16)
            wc[t, 0, some(r, s)] = head
            wc[t, 1, some(r, s)] = (total - head.astype(jnp.float32)).astype(jnp.bfloat16)
            for i in range(1, nrow):
                wc_out(t, s, i).start()

            @pl.when(source)
            def _():
                wr_ways(t, s, 0, True, start)
                wr_keep(t, s, 0).start()

        if t == 0:
            @pl.when(stays)
            def _():
                vt_in.wait()

            @pl.when(jnp.logical_not(stays))
            def _():
                vt_move.wait()

        for i in range(1, nrow):
            vt_out(t, i).start()
        if t:
            update_v(t - 1)
            for seat in range(ratio):
                update_w(t - 1, seat)

        @pl.when(source)
        def _():
            for s in range(splits):
                for i in range(1, nrow):
                    wc_in(t, s, (r + i) % nrow).wait()
                    wr_ways(t, s, i, True, start)
                    wr_keep(t, s, i).start()

        @pl.when(jnp.logical_not(source))
        def _():
            for s in range(splits):
                wr_in(t, s, j, r).wait()
                wr_ways(t, s, 0, False, start)
            for s in range(splits):
                for i in range(1, nrow):
                    wr_in(t, s, j, (r + i) % nrow).wait()
                    wr_ways(t, s, i, False, start)
            for s in range(splits):
                for i in range(1, nrow):
                    wc_in(t, s, (r + i) % nrow).wait()

        if last:
            update_v(t)
        else:
            v_relay(t + 1)
            b_ref[...] -= half * (dot(wc[t, 0], vr[t], NT) + dot(wc[t, 1], vr[t], NT))
            v_finish(t + 1)

        for i in range(1, nrow):
            vt_got(t, (r + i) % nrow).wait()

        @pl.when(source)
        def _():
            for s in range(splits):
                for i in range(nrow):
                    wr_keep(t, s, i).wait()

        for k in range(ratio):
            seat = (j + k) % ratio
            if k:
                for s in range(splits):
                    for i in range(nrow):
                        wr_in(t, s, seat, (r + i) % nrow).wait()
            if last:
                update_w(t, seat)
            else:
                turn_w(t, seat)
        mine = rows(c)
        w_ref[t] = wr[t, 0, mine].astype(jnp.float32) + wr[t, 1, mine].astype(jnp.float32)

    for t in range(ticks):
        for i in range(1, links):
            v_out(t, i).wait_send()
        for i in range(links):
            for k in range(1, ratio):
                v_side(t, i, k).wait_send()
        for i in range(1, nrow):
            vt_out(t, i).wait_send()
            for s in range(splits):
                rs_out(t, s, i).wait_send()
                wc_out(t, s, i).wait_send()

        @pl.when(source)
        def _():
            for s in range(splits):
                for i in range(nrow):
                    wr_ways(t, s, i, True, wait_send)

        @pl.when(jnp.logical_not(source))
        def _():
            for s in range(splits):
                for i in range(nrow):
                    wr_ways(t, s, i, False, wait_send)


def on_device(trailing, v_panels):
    nrow = lax.axis_size("row")
    ncol = lax.axis_size("col")
    rows_tile, cols_tile = trailing.shape
    ticks, piece, depth = v_panels.shape
    ratio = rows_tile // cols_tile
    links = ncol // ratio
    splits = SPLITS if piece % (SPLITS * 16) == 0 else 1
    scaling = 1.0 / math.sqrt(rows_tile * nrow)
    dma = pltpu.SemaphoreType.DMA
    vmem = pl.BlockSpec(memory_space=pltpu.VMEM)
    return pl.pallas_call(
        functools.partial(kernel, nrow, ncol, ratio, scaling),
        out_shape=(
            jax.ShapeDtypeStruct(trailing.shape, jnp.float32),
            jax.ShapeDtypeStruct(v_panels.shape, jnp.float32),
        ),
        in_specs=[vmem, vmem],
        out_specs=(vmem, vmem),
        scratch_shapes=[
            pltpu.VMEM((cols_tile, rows_tile), jnp.float32),
            pltpu.VMEM((ticks, rows_tile, depth), jnp.bfloat16),
            pltpu.VMEM((ticks, cols_tile, depth), jnp.bfloat16),
            pltpu.VMEM((ticks, cols_tile, depth), jnp.float32),
            pltpu.VMEM((ticks, cols_tile, depth), jnp.float32),
            pltpu.VMEM((ticks, 2, cols_tile, depth), jnp.bfloat16),
            pltpu.VMEM((ticks, 2, rows_tile, depth), jnp.bfloat16),
            dma((ticks, links)),
            dma((ticks, ncol)),
            dma,
            dma,
            dma((ticks, links + nrow, ratio)),
            dma((ticks, nrow)),
            dma((ticks, splits, nrow)),
            dma((ticks, splits, nrow)),
            dma((ticks, splits, nrow)),
            dma((ticks, splits, nrow)),
            dma((ticks, splits, nrow, ratio + 1)),
            dma((ticks, splits, ncol)),
            dma((ticks, splits, nrow)),
        ],
        compiler_params=pltpu.CompilerParams(collective_id=0, has_side_effects=True),
    )(trailing, v_panels)


def solution(mesh):
    in_specs = (P("row", "col"), P(None, ("row", "col"), None))
    out_specs = (P("row", "col"), P(None, ("row", "col"), None))
    return jax.shard_map(
        on_device, mesh=mesh, in_specs=in_specs, out_specs=out_specs, check_vma=False
    )
```

profile of v0, /device:TPU:6, one launch (start us, length us, event | category | flops | bytes accessed | tf_op | source)
XLA Modules:
  0.0 98.9 jit_solution(13643091574932612609)
XLA Ops:
  0.6 95.1 %shard_map.41 = (f32[768,384]{1,0:T(8,128)}, f32[3,96,256]{2,1,0:T(8,128)}) custom-call(f32[768,384]{1,0:T(8,128)} %a_ref.1, bf16[3,96,256]{2,1,0:T(8,128)(2,1)} %v_ref.1), custom_call_target="tpu_custom_call" | custom-call | tf_op jit(solution)/shard_map/pallas_call | solution.py:352
  95.8 0.0 copy-start
  95.8 2.4 %copy.6 = f32[768,384]{1,0:T(8,128)} copy(f32[768,384]{1,0:T(8,128)} %get-tuple-element.4) | data formatting | bytes 2359296
  98.2 0.0 copy-done
  98.2 0.7 copy.7
Async XLA Ops:
  95.8 2.4 %copy-start = (f32[3,96,256]{2,1,0:T(8,128)S(1)}, f32[3,96,256]{2,1,0:T(8,128)}, u32[]{:S(2)}) copy-start(f32[3,96,256]{2,1,0:T(8,128)} %get-tuple-element.5) | copy-start | bytes 884740
where the time goes:
time: 99.1 us; the launch traced here: 98.9 us
  Pallas kernels  95.1 us (96%)
  local copies, waits for them, and re-layouts  3.12 us (3%)
    pallas_call x1, Pallas kernels, on_device(): pl.pallas_call(functools.partial(kernel, nrow, ncol, ratio, scaling), out...  95.1 us
    unnamed x4, local copies, waits for them, and re-layouts  3.12 us

commit v1 on v0

v1 whole, which is shorter than its diff:
```python
import functools
import math

import jax
import jax.numpy as jnp
from jax import lax
from jax.experimental import pallas as pl
from jax.experimental.pallas import tpu as pltpu
from jax.sharding import PartitionSpec as P

MESH = pl.DeviceIdType.MESH
NT = (((1,), (1,)), ((), ()))
NN = (((1,), (0,)), ((), ()))
TN = (((0,), (0,)), ((), ()))
SPAN = 124.0
TINY = 1e-30
TILE = 16


def dot(a, b, dims):
    return lax.dot_general(a, b, dims, preferred_element_type=jnp.float32)


def halves(x):
    high = x.astype(jnp.bfloat16)
    return high, (x - high.astype(jnp.float32)).astype(jnp.bfloat16)


def dot2(a, b, dims):
    return dot(a[0], b[0], dims) + (dot(a[0], b[1], dims) + dot(a[1], b[0], dims))


def encode(ref, x):
    rows = x.shape[0]
    peak = jnp.maximum(jnp.max(jnp.abs(x), axis=0, keepdims=True), TINY).astype(jnp.bfloat16)
    ref[pl.ds(0, rows)] = jnp.exp2(x * (SPAN / peak.astype(jnp.float32))).astype(jnp.bfloat16)
    ref[pl.ds(ref.shape[0] - TILE, TILE)] = jnp.broadcast_to(peak, (TILE, x.shape[1]))


def decode(ref, rows):
    peak = ref[pl.ds(ref.shape[0] - TILE, TILE)].astype(jnp.float32)[:1]
    return jnp.log2(ref[pl.ds(0, rows)].astype(jnp.float32)) * (peak * (1.0 / SPAN))


def kernel(
    nrow, ncol, ratio, scaling,
    a_ref, v_ref, out_ref, w_ref,
    b_ref, vr, vt, part, sent, got, wcc, wrc, wc, wr, gp, ga, gb, gc, full,
    v_send, v_recv, vt_send, vt_recv, vx_send, vx_recv,
    rs_send, rs_recv, wc_send, wc_recv, wr_send, wr_recv, local_sem,
    ga_send, ga_recv, gb_send, gb_recv, gc_send, gc_recv, gd_send, gd_recv, ge_send, ge_recv,
):
    ticks, piece, depth = v_ref.shape
    rows_tile, cols_tile = a_ref.shape
    links = ncol // ratio
    pairs = full.shape[1]
    r = lax.axis_index("row")
    c = lax.axis_index("col")
    q = c // ratio
    j = c % ratio
    half = 0.5 * scaling
    share = depth // ratio
    slot = share // links

    def rows(at):
        return pl.ds(pl.multiple_of(at * piece, piece), piece)

    def remote(src, dst, send, recv, row, col):
        return pltpu.make_async_remote_copy(
            src_ref=src, dst_ref=dst, send_sem=send, recv_sem=recv,
            device_id=(row, col), device_id_type=MESH,
        )

    from_row, from_col = c // ratio, j * nrow + r
    to_row, to_col = c % nrow, r * ratio + c // nrow
    stays = jnp.logical_and(to_row == r, to_col == c)

    barrier = pltpu.get_barrier_semaphore()
    for i in range(1, nrow):
        pl.semaphore_signal(barrier, inc=1, device_id=((r + i) % nrow, c), device_id_type=MESH)
    for i in range(1, ncol):
        pl.semaphore_signal(barrier, inc=1, device_id=(r, (c + i) % ncol), device_id_type=MESH)

    @pl.when(jnp.logical_not(stays))
    def _():
        pl.semaphore_signal(barrier, inc=1, device_id=(from_row, from_col), device_id_type=MESH)
        pl.semaphore_signal(barrier, inc=1, device_id=(to_row, to_col), device_id_type=MESH)

    pl.semaphore_wait(barrier, nrow + ncol - 2 + jnp.where(stays, 0, 2))

    def v_out(t, i):
        return remote(
            v_ref.at[t], vr.at[t, rows(c)], v_send.at[t, i], v_recv.at[t, c],
            r, ((q + i) % links) * ratio + j,
        )

    def v_side(t, i, k):
        src_col = ((q + i) % links) * ratio + j
        src = v_ref.at[t] if i == 0 else vr.at[t, rows(src_col)]
        return remote(
            src, vr.at[t, rows(src_col)], vx_send.at[t, i, k - 1], v_recv.at[t, src_col],
            r, q * ratio + (j + k) % ratio,
        )

    def v_own(t):
        return pltpu.make_async_copy(v_ref.at[t], vr.at[t, rows(c)], v_recv.at[t, c])

    def v_in(t, col):
        return pltpu.make_async_copy(v_ref.at[t], vr.at[t, rows(col)], v_recv.at[t, col])

    def v_start(t):
        for i in range(1, links):
            v_out(t, i).start()
        for k in range(1, ratio):
            v_side(t, 0, k).start()
        v_own(t).start()

    vt_move = remote(v_ref, vt.at[:, rows(to_row)], vt_send, vt_recv, to_row, to_col)
    vt_in = pltpu.make_async_copy(v_ref, vt.at[:, rows(r)], vt_recv)

    v_start(0)

    @pl.when(stays)
    def _():
        vt_in.start()

    @pl.when(jnp.logical_not(stays))
    def _():
        vt_move.start()

    for t in range(1, ticks):
        v_start(t)

    b_ref[0], b_ref[1] = halves(a_ref[...].T)

    def v_relay(t):
        for i in range(1, links):
            v_in(t, ((q + i) % links) * ratio + j).wait()
            for k in range(1, ratio):
                v_side(t, i, k).start()

    def v_finish(t):
        v_in(t, c).wait()
        for i in range(links):
            for k in range(1, ratio):
                v_in(t, ((q + i) % links) * ratio + (j + k) % ratio).wait()

    def rs_out(t, i):
        peer = (r + i) % nrow
        return remote(
            sent.at[t, peer], got.at[t, r], rs_send.at[t, i], rs_recv.at[t, r], peer, c
        )

    def rs_in(t, peer):
        return pltpu.make_async_copy(sent.at[t, peer], got.at[t, peer], rs_recv.at[t, peer])

    def wc_out(t, i):
        peer = (r + i) % nrow
        spot = wcc.at[t, r]
        return remote(spot, spot, wc_send.at[t, i], wc_recv.at[t, r], peer, c)

    def wc_in(t, peer):
        spot = wcc.at[t, peer]
        return pltpu.make_async_copy(spot, spot, wc_recv.at[t, peer])

    def vt_out(t, i):
        peer = (r + i) % nrow
        spot = vt.at[t, rows(r)]
        return remote(spot, spot, vx_send.at[t, links + i - 1, 0], vx_recv.at[t, r], peer, c)

    def vt_got(t, peer):
        spot = vt.at[t, rows(peer)]
        return pltpu.make_async_copy(spot, spot, vx_recv.at[t, peer])

    source = q == r
    up = jnp.logical_and(q >= r, q < links - 1)
    down = jnp.logical_and(q <= r, q > 0)

    def wr_out(t, i, way, first):
        peer = (r + i) % nrow
        at = j * nrow + peer
        spot = wrc.at[t, at]
        src = wcc.at[t, peer] if first else spot
        if way == 0:
            col = c + ratio
        elif way == 1:
            col = c - ratio
        else:
            col = q * ratio + (j + way - 1) % ratio
        return remote(src, spot, wr_send.at[t, i, way], wr_recv.at[t, at], r, col)

    def wr_in(t, seat, peer):
        at = seat * nrow + peer
        spot = wrc.at[t, at]
        return pltpu.make_async_copy(spot, spot, wr_recv.at[t, at])

    def wr_keep(t, i):
        peer = (r + i) % nrow
        return pltpu.make_async_copy(
            wcc.at[t, peer], wrc.at[t, j * nrow + peer], local_sem.at[t, i]
        )

    def wr_ways(t, i, first, act):
        @pl.when(up)
        def _():
            act(wr_out(t, i, 0, first))

        @pl.when(down)
        def _():
            act(wr_out(t, i, 1, first))

        for k in range(1, ratio):
            act(wr_out(t, i, 1 + k, first))

    def start(copy):
        copy.start()

    def wait_send(copy):
        copy.wait_send()

    def partial(t):
        v_relay(t)
        v_finish(t)
        part[t] = dot(b_ref[0], vr[t], NN) + dot(b_ref[1], vr[t], NN)
        for i in range(1, nrow):
            peer = (r + i) % nrow
            encode(sent.at[t, peer], part[t, rows(peer)])
            rs_out(t, i).start()

    def collect(t):
        total = part[t, rows(r)]
        for i in range(1, nrow):
            peer = (r + i) % nrow
            rs_in(t, peer).wait()
            total = total + decode(got.at[t, peer], piece)
        encode(wcc.at[t, r], total * scaling)
        for i in range(1, nrow):
            wc_out(t, i).start()

        @pl.when(source)
        def _():
            wr_ways(t, 0, True, start)
            wr_keep(t, 0).start()

    def relay(t):
        @pl.when(source)
        def _():
            for i in range(1, nrow):
                wc_in(t, (r + i) % nrow).wait()
                wr_ways(t, i, True, start)
                wr_keep(t, i).start()

        @pl.when(jnp.logical_not(source))
        def _():
            for i in range(nrow):
                wr_in(t, j, (r + i) % nrow).wait()
                wr_ways(t, i, False, start)
            for i in range(1, nrow):
                wc_in(t, (r + i) % nrow).wait()

    def open_cols(t):
        for k in range(nrow):
            wc[t, 0, pl.ds(k * piece, piece)], wc[t, 1, pl.ds(k * piece, piece)] = halves(
                decode(wcc.at[t, k], piece)
            )

    def open_rows(t):
        @pl.when(source)
        def _():
            for i in range(nrow):
                wr_keep(t, i).wait()

        for k in range(1, ratio):
            for i in range(nrow):
                wr_in(t, (j + k) % ratio, (r + i) % nrow).wait()
        for k in range(ratio * nrow):
            wr[t, 0, pl.ds(k * piece, piece)], wr[t, 1, pl.ds(k * piece, piece)] = halves(
                decode(wrc.at[t, k], piece)
            )

    owner = r < pairs
    first = r // 2
    later = (r + 3) // 2

    def shares(at):
        return pl.ds(pl.multiple_of(at * share, share), share)

    def slots(at):
        return pl.ds(pl.multiple_of(at * slot, slot), slot)

    def ga_out(k, s):
        to = (j + s) % ratio
        return remote(
            gp.at[k, shares(to)], ga.at[k, j], ga_send.at[k, s], ga_recv.at[k, j],
            r, q * ratio + to,
        )

    def ga_in(k, s):
        at = (j + s) % ratio
        return pltpu.make_async_copy(ga.at[k, at], ga.at[k, at], ga_recv.at[k, at])

    def gb_out(k, s):
        to = (q + s) % links
        return remote(
            gb.at[k, slots(to)], gc.at[k, q], gb_send.at[k, s], gb_recv.at[k, q],
            r, to * ratio + j,
        )

    def gb_in(k, s):
        at = (q + s) % links
        return pltpu.make_async_copy(gc.at[k, at], gc.at[k, at], gb_recv.at[k, at])

    def final(k, at):
        return full.at[k, r, pl.ds(pl.multiple_of(j * share + at * slot, slot), slot)]

    def gc_out(k, s):
        to = (q + s) % links
        return remote(
            final(k, q), final(k, q), gc_send.at[k, s], gc_recv.at[k, q], r, to * ratio + j
        )

    def gc_in(k, s):
        at = (q + s) % links
        return pltpu.make_async_copy(final(k, at), final(k, at), gc_recv.at[k, at])

    def gd_out(k, i):
        spot = full.at[k, r, shares(j)]
        return remote(spot, spot, gd_send.at[k, i], gd_recv.at[k, r], (r + i) % nrow, c)

    def gd_in(k, m):
        spot = full.at[k, m, shares(j)]
        return pltpu.make_async_copy(spot, spot, gd_recv.at[k, m])

    def ge_out(k, s):
        spot = full.at[k, :, shares(j)]
        return remote(
            spot, spot, ge_send.at[k, s], ge_recv.at[k, j], r, q * ratio + (j + s) % ratio
        )

    def ge_in(k, s):
        at = (j + s) % ratio
        spot = full.at[k, :, shares(at)]
        return pltpu.make_async_copy(spot, spot, ge_recv.at[k, at])

    def gram_a(k):
        @pl.when(owner)
        def _():
            if k:
                gp[k] = dot(wc[first, 0], vt[later], TN) + dot(wc[first, 1], vt[later], TN)
            else:
                gp[k] = dot(vt[first], vt[later], TN)
            for s in range(1, ratio):
                ga_out(k, s).start()

    def gram_b(k):
        @pl.when(owner)
        def _():
            total = gp[k, shares(j)]
            for s in range(1, ratio):
                ga_in(k, s).wait()
                total = total + ga[k, (j + s) % ratio]
            gb[k] = total
            for s in range(1, links):
                gb_out(k, s).start()

    def gram_c(k):
        @pl.when(owner)
        def _():
            total = gb[k, slots(q)]
            for s in range(1, links):
                gb_in(k, s).wait()
                total = total + gc[k, (q + s) % links]
            full[k, r, pl.ds(pl.multiple_of(j * share + q * slot, slot), slot)] = total
            for s in range(1, links):
                gc_out(k, s).start()

    def gram_d(k):
        @pl.when(owner)
        def _():
            for s in range(1, links):
                gc_in(k, s).wait()
            for i in range(1, nrow):
                gd_out(k, i).start()

    def gram_e(k):
        for m in range(pairs):
            @pl.when(r != m)
            def _():
                gd_in(k, m).wait()
        for s in range(1, ratio):
            ge_out(k, s).start()

    def gram_f(k):
        for s in range(1, ratio):
            ge_in(k, s).wait()

    partial(0)
    partial(1)

    @pl.when(stays)
    def _():
        vt_in.wait()

    @pl.when(jnp.logical_not(stays))
    def _():
        vt_move.wait()

    for t in range(ticks):
        for i in range(1, nrow):
            vt_out(t, i).start()

    collect(0)
    partial(2)
    collect(1)
    relay(0)
    for t in range(ticks):
        for i in range(1, nrow):
            vt_got(t, (r + i) % nrow).wait()
    gram_a(0)
    open_cols(0)
    collect(2)
    gram_b(0)
    relay(1)
    open_cols(1)
    gram_a(1)
    gram_c(0)
    gram_b(1)
    gram_d(0)
    open_rows(0)

    def update(t):
        out_ref[...] = (out_ref if t else a_ref)[...] - half * (
            dot(vr[t], wc[t, 0], NT) + dot(vr[t], wc[t, 1], NT)
            + dot(wr[t, 0], vt[t], NT) + dot(wr[t, 1], vt[t], NT)
        )

    gram_c(1)
    relay(2)
    gram_e(0)
    gram_d(1)
    update(0)
    open_rows(1)
    open_cols(2)
    gram_f(0)
    gram_e(1)
    gram_f(1)
    fix = scaling * half
    g01, g02, g12 = (halves(full[0, m]) for m in range(3))
    n01, n02 = (halves(full[1, m]) for m in range(2))
    k12 = halves(full[1, 2] - fix * (dot2(n01, g02, TN) + dot2(g01, n02, TN)))

    def one(v, x):
        base = x[1, 0].astype(jnp.float32) + x[1, 1].astype(jnp.float32)
        return base - fix * (
            dot(v[0], n01[0], NN) + dot(v[0], n01[1], NN)
            + dot2((x[0, 0], x[0, 1]), g01, NN)
        )

    def two(v, x):
        base = x[2, 0].astype(jnp.float32) + x[2, 1].astype(jnp.float32)
        return base - fix * (
            dot(v[0], n02[0], NN) + dot(v[0], n02[1], NN)
            + dot2((x[0, 0], x[0, 1]), g02, NN)
            + dot(v[1], k12[0], NN) + dot(v[1], k12[1], NN)
            + dot2((x[1, 0], x[1, 1]), g12, NN)
        )

    wc[1, 0], wc[1, 1] = halves(one(vt, wc))
    wr[1, 0], wr[1, 1] = halves(one(vr, wr))
    update(1)
    wc[2, 0], wc[2, 1] = halves(two(vt, wc))
    open_rows(2)
    wr[2, 0], wr[2, 1] = halves(two(vr, wr))
    update(2)
    mine = rows(c)
    for t in range(ticks):
        w_ref[t] = wr[t, 0, mine].astype(jnp.float32) + wr[t, 1, mine].astype(jnp.float32)

    for t in range(ticks):
        for i in range(1, links):
            v_out(t, i).wait_send()
        for i in range(links):
            for k in range(1, ratio):
                v_side(t, i, k).wait_send()
        for i in range(1, nrow):
            vt_out(t, i).wait_send()
            rs_out(t, i).wait_send()
            wc_out(t, i).wait_send()

        @pl.when(source)
        def _():
            for i in range(nrow):
                wr_ways(t, i, True, wait_send)

        @pl.when(jnp.logical_not(source))
        def _():
            for i in range(nrow):
                wr_ways(t, i, False, wait_send)

    for k in range(2):
        @pl.when(owner)
        def _():
            for s in range(1, ratio):
                ga_out(k, s).wait_send()
            for s in range(1, links):
                gb_out(k, s).wait_send()
                gc_out(k, s).wait_send()
            for i in range(1, nrow):
                gd_out(k, i).wait_send()

        for s in range(1, ratio):
            ge_out(k, s).wait_send()


def on_device(trailing, v_panels):
    nrow = lax.axis_size("row")
    ncol = lax.axis_size("col")
    rows_tile, cols_tile = trailing.shape
    ticks, piece, depth = v_panels.shape
    ratio = rows_tile // cols_tile
    links = ncol // ratio
    scaling = 1.0 / math.sqrt(rows_tile * nrow)
    pairs = ticks * (ticks - 1) // 2
    coded = -(-piece // TILE) * TILE + TILE
    share = depth // ratio
    dma = pltpu.SemaphoreType.DMA
    vmem = pl.BlockSpec(memory_space=pltpu.VMEM)
    f32, bf16 = jnp.float32, jnp.bfloat16
    return pl.pallas_call(
        functools.partial(kernel, nrow, ncol, ratio, scaling),
        out_shape=(
            jax.ShapeDtypeStruct(trailing.shape, f32),
            jax.ShapeDtypeStruct(v_panels.shape, f32),
        ),
        in_specs=[vmem, vmem],
        out_specs=(vmem, vmem),
        scratch_shapes=[
            pltpu.VMEM((2, cols_tile, rows_tile), bf16),
            pltpu.VMEM((ticks, rows_tile, depth), bf16),
            pltpu.VMEM((ticks, cols_tile, depth), bf16),
            pltpu.VMEM((ticks, cols_tile, depth), f32),
            pltpu.VMEM((ticks, nrow, coded, depth), bf16),
            pltpu.VMEM((ticks, nrow, coded, depth), bf16),
            pltpu.VMEM((ticks, nrow, coded, depth), bf16),
            pltpu.VMEM((ticks, ratio * nrow, coded, depth), bf16),
            pltpu.VMEM((ticks, 2, cols_tile, depth), bf16),
            pltpu.VMEM((ticks, 2, rows_tile, depth), bf16),
            pltpu.VMEM((2, depth, depth), f32),
            pltpu.VMEM((2, ratio, share, depth), f32),
            pltpu.VMEM((2, share, depth), f32),
            pltpu.VMEM((2, links, share // links, depth), f32),
            pltpu.VMEM((2, pairs, depth, depth), f32),
            dma((ticks, links)),
            dma((ticks, ncol)),
            dma,
            dma,
            dma((ticks, links + nrow, ratio)),
            dma((ticks, nrow)),
            dma((ticks, nrow)),
            dma((ticks, nrow)),
            dma((ticks, nrow)),
            dma((ticks, nrow)),
            dma((ticks, nrow, ratio + 1)),
            dma((ticks, ncol)),
            dma((ticks, nrow)),
            dma((2, ratio)), dma((2, ratio)),
            dma((2, links)), dma((2, links)),
            dma((2, links)), dma((2, links)),
            dma((2, nrow)), dma((2, nrow)),
            dma((2, ratio)), dma((2, ratio)),
        ],
        compiler_params=pltpu.CompilerParams(
            collective_id=0, has_side_effects=True, vmem_limit_bytes=48 * 1024 * 1024
        ),
    )(trailing, v_panels)


def solution(mesh):
    in_specs = (P("row", "col"), P(None, ("row", "col"), None))
    out_specs = (P("row", "col"), P(None, ("row", "col"), None))
    return jax.shard_map(
        on_device, mesh=mesh, in_specs=in_specs, out_specs=out_specs, check_vma=False
    )
```

time: 99.1 us -> 93.8 us (0.947)
  the two profiles are of different devices: /device:TPU:6 before, /device:TPU:27 now
where the time goes in v1:
time: 93.8 us; the launch traced here: 92.3 us
  Pallas kernels  87.7 us (93%)
  local copies, waits for them, and re-layouts  3.9 us (4%)
    pallas_call x1, Pallas kernels, on_device(): pl.pallas_call(functools.partial(kernel, nrow, ncol, ratio, scaling), out...  87.7 us
    unnamed x6, local copies, waits for them, and re-layouts  3.9 us

profile of v1, /device:TPU:27, one launch (start us, length us, event | category | flops | bytes accessed | tf_op | source)
XLA Modules:
  0.0 92.3 jit_solution(9591296438622692610)
XLA Ops:
  0.6 0.0 copy-start
  0.6 1.3 %copy-done = f32[768,384]{1,0:T(8,128)S(1)} copy-done((f32[768,384]{1,0:T(8,128)S(1)}, f32[768,384]{1,0:T(8,128)}, u32[]{:S(2)}) %copy-start) | copy-done | bytes 1179672
  1.9 0.0 copy-start.1
  1.9 0.9 copy-done.1
  2.8 87.7 %shard_map.41 = (f32[768,384]{1,0:T(8,128)S(1)}, f32[3,96,256]{2,1,0:T(8,128)S(1)}) custom-call(f32[768,384]{1,0:T(8,128)S(1)} %copy-done, bf16[3,96,256]{2,1,0:T(8,128)(2,1)S(1)} %copy-done.1), custom_call_target="tpu_custom_call" | custom-call | tf_op jit(solution)/shard_map/pallas_call | solution.py:529
  90.5 1.0 %copy.6 = f32[768,384]{1,0:T(8,128)} copy(f32[768,384]{1,0:T(8,128)S(1)} %get-tuple-element.4) | data formatting | bytes 2359296
  91.6 0.7 copy.7
Async XLA Ops:
  0.6 1.3 %copy-start = (f32[768,384]{1,0:T(8,128)S(1)}, f32[768,384]{1,0:T(8,128)}, u32[]{:S(2)}) copy-start(f32[768,384]{1,0:T(8,128)} %a_ref.1) | copy-start | bytes 3538948
  1.9 0.9 copy-start.1

commit v2 on v1

v2 whole, which is shorter than its diff:
```python
import functools
import math

import jax
import jax.numpy as jnp
from jax import lax
from jax.experimental import pallas as pl
from jax.experimental.pallas import tpu as pltpu
from jax.sharding import PartitionSpec as P

MESH = pl.DeviceIdType.MESH
NT = (((1,), (1,)), ((), ()))
NN = (((1,), (0,)), ((), ()))
TN = (((0,), (0,)), ((), ()))
SPAN = 124.0
TINY = 1e-30
TILE = 8


def dot(a, b, dims):
    return lax.dot_general(a, b, dims, preferred_element_type=jnp.float32)


def halves(x):
    high = x.astype(jnp.bfloat16)
    return high, (x - high.astype(jnp.float32)).astype(jnp.bfloat16)


def dot2(a, b, dims):
    return dot(a[0], b[0], dims) + (dot(a[0], b[1], dims) + dot(a[1], b[0], dims))


def dot3(a, b, dims):
    return dot(a, b[0], dims) + dot(a, b[1], dims)


def dot4(a, b, dims):
    return dot(a[0], b, dims) + dot(a[1], b, dims)


def encode(ref, x):
    rows = x.shape[0]
    peak = jnp.maximum(jnp.max(jnp.abs(x), axis=0, keepdims=True), TINY).astype(jnp.bfloat16)
    ref[pl.ds(0, rows)] = jnp.exp2(x * (SPAN / peak.astype(jnp.float32))).astype(jnp.bfloat16)
    ref[pl.ds(ref.shape[0] - TILE, TILE)] = jnp.broadcast_to(peak, (TILE, x.shape[1]))


def decode(ref, rows):
    peak = ref[pl.ds(ref.shape[0] - TILE, TILE)].astype(jnp.float32)[:1]
    return jnp.log2(ref[pl.ds(0, rows)].astype(jnp.float32)) * (peak * (1.0 / SPAN))


def kernel(
    nrow, ncol, ratio, scaling,
    a_hbm, v_ref, out_ref, w_ref,
    a_ref, ab, vr, vt, vtt, part, sent, got, own, wcc, wrc, wct, wr, zt, gp, ga, gs, gc, gq, gram, fact,
    v_send, v_recv, vt_send, vt_recv, vx_send, vo_send, vx_recv,
    rs_send, rs_recv, wc_send, wc_recv, wr_send, wr_recv, wx_send, wx_recv, local_sem, in_sem,
    ga_send, ga_recv, gb_send, gb_recv, gd_send, gd_recv, ge_send, ge_recv,
):
    ticks, piece, depth = v_ref.shape
    rows_tile, cols_tile = a_hbm.shape
    links = ncol // ratio
    chosen = [(u, t) for t in range(ticks) for u in range(t)]
    pairs = len(chosen)
    r = lax.axis_index("row")
    c = lax.axis_index("col")
    q = c // ratio
    j = c % ratio
    half = 0.5 * scaling
    fix = scaling * half
    strip = depth // nrow
    thin = strip // ratio

    def rows(at):
        return pl.ds(pl.multiple_of(at * piece, piece), piece)

    def strips(at):
        return pl.ds(pl.multiple_of(at * strip, strip), strip)

    def thins(at):
        return pl.ds(pl.multiple_of(at * thin, thin), thin)

    def remote(src, dst, send, recv, row, col):
        return pltpu.make_async_remote_copy(
            src_ref=src, dst_ref=dst, send_sem=send, recv_sem=recv,
            device_id=(row, col), device_id_type=MESH,
        )

    from_row, from_col = c // ratio, j * nrow + r
    to_row, to_col = c % nrow, r * ratio + c // nrow
    stays = jnp.logical_and(to_row == r, to_col == c)

    a_in = pltpu.make_async_copy(a_hbm, a_ref, in_sem.at[0])
    v_own = pltpu.make_async_copy(v_ref, vr.at[:, rows(c)], in_sem.at[1])
    v_own.start()
    a_in.start()
    barrier = pltpu.get_barrier_semaphore()

    def greet(row, col):
        pl.semaphore_signal(barrier, inc=1, device_id=(row, col), device_id_type=MESH)

    for i in range(1, nrow):
        greet((r + i) % nrow, c)
    for k in range(1, ratio):
        greet(r, q * ratio + (j + k) % ratio)
    for i in range(1, links):
        greet(r, ((q + i) % links) * ratio + j)

    @pl.when(jnp.logical_not(stays))
    def _():
        greet(from_row, from_col)
        greet(to_row, to_col)

    v_own.wait()
    pl.semaphore_wait(barrier, nrow + ratio + links - 3 + jnp.where(stays, 0, 2))

    def v_out(t, i):
        spot = vr.at[t, rows(c)]
        return remote(
            spot, spot, v_send.at[t, i], v_recv.at[t, c], r, ((q + i) % links) * ratio + j
        )

    def v_side(t, i, k):
        at = ((q + i) % links) * ratio + j
        spot = vr.at[t, rows(at)]
        return remote(
            spot, spot, vx_send.at[t, i, k - 1], v_recv.at[t, at],
            r, q * ratio + (j + k) % ratio,
        )

    def v_in(t, col):
        spot = vr.at[t, rows(col)]
        return pltpu.make_async_copy(spot, spot, v_recv.at[t, col])

    vt_move = remote(v_ref, vt.at[:, rows(to_row)], vt_send, vt_recv, to_row, to_col)
    vt_in = pltpu.make_async_copy(v_ref, vt.at[:, rows(r)], vt_recv)

    def vt_out(t, i):
        peer = (r + i) % nrow
        spot = vt.at[t, rows(r)]
        return remote(spot, spot, vo_send.at[t, i], vx_recv.at[t, r], peer, c)

    def vt_got(t, peer):
        spot = vt.at[t, rows(peer)]
        return pltpu.make_async_copy(spot, spot, vx_recv.at[t, peer])

    def v_gather(t):
        for i in range(1, links):
            v_in(t, ((q + i) % links) * ratio + j).wait()
            for k in range(1, ratio):
                v_side(t, i, k).start()
        for i in range(links):
            for k in range(1, ratio):
                v_in(t, ((q + i) % links) * ratio + (j + k) % ratio).wait()

    def vt_spread():
        @pl.when(stays)
        def _():
            vt_in.wait()

        @pl.when(jnp.logical_not(stays))
        def _():
            vt_move.wait()

        for t in range(ticks):
            for i in range(1, nrow):
                vt_out(t, i).start()

    def vt_close():
        for t in range(ticks):
            for i in range(1, nrow):
                vt_got(t, (r + i) % nrow).wait()
            vtt[t] = vt[t].astype(jnp.float32).T.astype(jnp.bfloat16)

    def rs_out(t, i):
        peer = (r + i) % nrow
        return remote(
            sent.at[t, peer], got.at[t, r], rs_send.at[t, i], rs_recv.at[t, r], peer, c
        )

    def rs_in(t, peer):
        return pltpu.make_async_copy(sent.at[t, peer], got.at[t, peer], rs_recv.at[t, peer])

    def wc_out(t, i):
        spot = wcc.at[t, r]
        return remote(spot, spot, wc_send.at[t, i], wc_recv.at[t, r], (r + i) % nrow, c)

    def wc_in(t, peer):
        spot = wcc.at[t, peer]
        return pltpu.make_async_copy(spot, spot, wc_recv.at[t, peer])

    source = q == r

    def wr_out(t, i):
        return remote(
            wcc.at[t, r], wrc.at[t, j, r], wr_send.at[t, i], wr_recv.at[t, r],
            q, ((q + i) % links) * ratio + j,
        )

    def wr_in(t, peer):
        spot = wrc.at[t, j, peer]
        return pltpu.make_async_copy(spot, spot, wr_recv.at[t, peer])

    def wr_keep(t):
        return pltpu.make_async_copy(wcc.at[t], wrc.at[t, j], local_sem.at[t])

    def wx_out(t, k):
        spot = wrc.at[t, j]
        return remote(
            spot, spot, wx_send.at[t, k], wx_recv.at[t, j], r, q * ratio + (j + k) % ratio
        )

    def wx_in(t, k):
        at = (j + k) % ratio
        spot = wrc.at[t, at]
        return pltpu.make_async_copy(spot, spot, wx_recv.at[t, at])

    def partial(t):
        v_gather(t)
        part[t] = dot(vr[t], ab[0], TN) + dot(vr[t], ab[1], TN)
        for i in range(1, nrow):
            peer = (r + i) % nrow
            encode(sent.at[t, peer], part[t, strips(peer)])
            rs_out(t, i).start()

    def collect(t):
        total = part[t, strips(r)]
        for i in range(1, nrow):
            peer = (r + i) % nrow
            rs_in(t, peer).wait()
            total = total + decode(got.at[t, peer], strip)
        total = total * scaling
        encode(wcc.at[t, r], total)
        for i in range(1, nrow):
            wc_out(t, i).start()
        for i in range(1, links):
            wr_out(t, i).start()
        own[t, 0], own[t, 1] = halves(total)

    def relay(t):
        for i in range(1, nrow):
            wc_in(t, (r + i) % nrow).wait()

        @pl.when(source)
        def _():
            wr_keep(t).start()
            wr_keep(t).wait()

        @pl.when(jnp.logical_not(source))
        def _():
            for i in range(nrow):
                wr_in(t, (r + i) % nrow).wait()

        for k in range(1, ratio):
            wx_out(t, k).start()

    def open_cols(t):
        for k in range(nrow):
            at = pl.ds(k * strip, strip)
            wct[t, 0, at], wct[t, 1, at] = halves(decode(wcc.at[t, k], strip))

    def open_rows(t):
        for k in range(1, ratio):
            wx_in(t, k).wait()
        for s in range(ratio):
            x = jnp.concatenate([decode(wrc.at[t, s, k], strip) for k in range(nrow)], axis=0)
            at = pl.ds(s * cols_tile, cols_tile)
            wr[t, 0, at], wr[t, 1, at] = halves(x.T)

    def ga_out(k, s):
        to = (j + s) % ratio
        return remote(
            gp.at[k, :, thins(to)], ga.at[k, j], ga_send.at[k, s], ga_recv.at[k, j],
            r, q * ratio + to,
        )

    def ga_in(k, s):
        at = (j + s) % ratio
        return pltpu.make_async_copy(ga.at[k, at], ga.at[k, at], ga_recv.at[k, at])

    def gb_out(k, s):
        return remote(
            gs.at[k], gc.at[k, q], gb_send.at[k, s], gb_recv.at[k, q],
            r, ((q + s) % links) * ratio + j,
        )

    def gb_in(k, s):
        at = (q + s) % links
        return pltpu.make_async_copy(gc.at[k, at], gc.at[k, at], gb_recv.at[k, at])

    def gd_out(k, i):
        spot = gq.at[k, j, r]
        return remote(spot, spot, gd_send.at[k, i], gd_recv.at[k, r], (r + i) % nrow, c)

    def gd_in(k, i):
        at = (r + i) % nrow
        spot = gq.at[k, j, at]
        return pltpu.make_async_copy(spot, spot, gd_recv.at[k, at])

    def ge_out(k, s):
        spot = gq.at[k, j]
        return remote(
            spot, spot, ge_send.at[k, s], ge_recv.at[k, j], r, q * ratio + (j + s) % ratio
        )

    def ge_in(k, s):
        at = (j + s) % ratio
        spot = gq.at[k, at]
        return pltpu.make_async_copy(spot, spot, ge_recv.at[k, at])

    def gram_a(k):
        for m, (u, t) in enumerate(chosen):
            gp[k, m] = dot4(own.at[u], vt[t], NN) if k else dot(vtt[u, strips(r)], vt[t], NN)
        for s in range(1, ratio):
            ga_out(k, s).start()

    def gram_b(k):
        for s in range(1, ratio):
            ga_in(k, s).wait()
        for m in range(pairs):
            total = gp[k, m, thins(j)]
            for s in range(1, ratio):
                total = total + ga[k, (j + s) % ratio, m]
            gp[k, m, thins(j)] = total
            encode(gs.at[k, m], total)
        for s in range(1, links):
            gb_out(k, s).start()

    def gram_d(k):
        for s in range(1, links):
            gb_in(k, s).wait()
        for m in range(pairs):
            total = gp[k, m, thins(j)]
            for s in range(1, links):
                total = total + decode(gc.at[k, (q + s) % links, m], thin)
            encode(gq.at[k, j, r, m], total)
        for i in range(1, nrow):
            gd_out(k, i).start()

    def gram_e(k):
        for i in range(1, nrow):
            gd_in(k, i).wait()
        for s in range(1, ratio):
            ge_out(k, s).start()

    def gram_f(k):
        for s in range(1, ratio):
            ge_in(k, s).wait()
        for m in range(pairs):
            for i in range(nrow):
                for s in range(ratio):
                    at = pl.ds(i * strip + s * thin, thin)
                    gram[k, m, at] = decode(gq.at[k, s, i, m], thin)

    def keep(k, m, x):
        fact[k, m, 0], fact[k, m, 1] = halves(x)

    def kept(k, m):
        return fact[k, m, 0], fact[k, m, 1]

    def make_c():
        keep(0, 0, -fix * gram[0, 0])
        keep(0, 2, -fix * gram[0, 2])
        keep(0, 1, dot2(kept(0, 0), kept(0, 2), NN) - fix * gram[0, 1])

    def make_d():
        keep(1, 0, -fix * gram[1, 0])
        keep(1, 1, dot2(kept(1, 0), kept(0, 2), NN) - fix * gram[1, 1])
        last = (
            gram[1, 2]
            + dot2(kept(0, 0), halves(gram[1, 1]), TN)
            + dot2(kept(1, 0), halves(gram[0, 1]), TN)
        )
        keep(1, 2, -fix * last)

    def both(x):
        return x[0], x[1]

    def full(x):
        return x[0].astype(jnp.float32) + x[1].astype(jnp.float32)

    def make_z():
        zt[0, 0], zt[0, 1] = halves(
            vtt[0].astype(jnp.float32)
            + dot4(kept(0, 0), vtt[1], NN) + dot4(kept(0, 1), vtt[2], NN)
        )
        zt[1, 0], zt[1, 1] = halves(vtt[1].astype(jnp.float32) + dot4(kept(0, 2), vtt[2], NN))

    def minus(terms):
        out_ref[...] = out_ref[...] - half * terms


    for t in range(ticks):
        if t == 1:
            @pl.when(stays)
            def _():
                vt_in.start()

            @pl.when(jnp.logical_not(stays))
            def _():
                vt_move.start()
        for i in range(1, links):
            v_out(t, i).start()
        for k in range(1, ratio):
            v_side(t, 0, k).start()

    a_in.wait()
    ab[0], ab[1] = halves(a_ref[...])

    partial(0)
    vt_spread()
    partial(1)
    collect(0)
    vt_close()
    gram_a(0)
    collect(1)
    gram_a(1)
    gram_b(0)
    gram_b(1)
    partial(2)
    relay(0)
    open_cols(0)
    gram_d(0)
    collect(2)
    gram_d(1)
    relay(1)
    open_cols(1)
    gram_e(0)
    open_rows(0)
    gram_e(1)
    gram_f(0)
    make_c()
    make_z()
    out_ref[...] = a_ref[...]
    minus(dot2(both(wr.at[0]), both(zt.at[0]), NN))
    relay(2)
    open_cols(2)
    open_rows(1)
    minus(dot2(both(wr.at[1]), both(zt.at[1]), NN))
    one = full(wct.at[1]) + dot2(kept(0, 0), both(wct.at[0]), TN)
    two = (
        full(wct.at[2]) + dot2(kept(0, 1), both(wct.at[0]), TN)
        + dot2(kept(0, 2), both(wct.at[1]), TN)
    )
    part[1] = one
    part[2] = two
    gram_f(1)
    make_d()
    zero = full(wct.at[0]) + dot4(kept(1, 0), vtt[1], NN) + dot4(kept(1, 1), vtt[2], NN)
    minus(dot3(vr[0], halves(zero), NN))
    one = part[1] + dot4(kept(1, 0), vtt[0], TN) + dot4(kept(1, 2), vtt[2], NN)
    minus(dot3(vr[1], halves(one), NN))
    two = part[2] + dot4(kept(1, 1), vtt[0], TN) + dot4(kept(1, 2), vtt[1], TN)
    minus(dot3(vr[2], halves(two), NN))
    open_rows(2)
    minus(dot4(both(wr.at[2]), vtt[2], NN))
    mine = rows(c)
    for t in range(ticks):
        total = wr[t, 0, mine].astype(jnp.float32) + wr[t, 1, mine].astype(jnp.float32)
        for m, (u, later) in enumerate(chosen):
            if later == t:
                total = total + dot2((wr[u, 0, mine], wr[u, 1, mine]), kept(0, m), NN)
                total = total + dot3(vr[u, mine], kept(1, m), NN)
        w_ref[t] = total

    for t in range(ticks):
        for i in range(1, links):
            v_out(t, i).wait_send()
            wr_out(t, i).wait_send()
        for k in range(1, ratio):
            for i in range(links):
                v_side(t, i, k).wait_send()
            wx_out(t, k).wait_send()
        for i in range(1, nrow):
            vt_out(t, i).wait_send()
            rs_out(t, i).wait_send()
            wc_out(t, i).wait_send()

    for k in range(2):
        for s in range(1, ratio):
            ga_out(k, s).wait_send()
            ge_out(k, s).wait_send()
        for s in range(1, links):
            gb_out(k, s).wait_send()
        for i in range(1, nrow):
            gd_out(k, i).wait_send()


def on_device(trailing, v_panels):
    nrow = lax.axis_size("row")
    ncol = lax.axis_size("col")
    rows_tile, cols_tile = trailing.shape
    ticks, piece, depth = v_panels.shape
    ratio = rows_tile // cols_tile
    links = ncol // ratio
    scaling = 1.0 / math.sqrt(rows_tile * nrow)
    pairs = ticks * (ticks - 1) // 2
    strip = depth // nrow
    thin = strip // ratio
    dma = pltpu.SemaphoreType.DMA
    vmem = pl.BlockSpec(memory_space=pltpu.VMEM)
    f32, bf16 = jnp.float32, jnp.bfloat16
    return pl.pallas_call(
        functools.partial(kernel, nrow, ncol, ratio, scaling),
        out_shape=(
            jax.ShapeDtypeStruct(trailing.shape, f32),
            jax.ShapeDtypeStruct(v_panels.shape, f32),
        ),
        in_specs=[pl.BlockSpec(memory_space=pltpu.MemorySpace.HBM)] * 2,
        out_specs=(vmem, vmem),
        scratch_shapes=[
            pltpu.VMEM((rows_tile, cols_tile), f32),
            pltpu.VMEM((2, rows_tile, cols_tile), bf16),
            pltpu.VMEM((ticks, rows_tile, depth), bf16),
            pltpu.VMEM((ticks, cols_tile, depth), bf16),
            pltpu.VMEM((ticks, depth, cols_tile), bf16),
            pltpu.VMEM((ticks, depth, cols_tile), f32),
            pltpu.VMEM((ticks, nrow, strip + TILE, cols_tile), bf16),
            pltpu.VMEM((ticks, nrow, strip + TILE, cols_tile), bf16),
            pltpu.VMEM((ticks, 2, strip, cols_tile), bf16),
            pltpu.VMEM((ticks, nrow, strip + TILE, cols_tile), bf16),
            pltpu.VMEM((ticks, ratio, nrow, strip + TILE, cols_tile), bf16),
            pltpu.VMEM((ticks, 2, depth, cols_tile), bf16),
            pltpu.VMEM((ticks, 2, rows_tile, depth), bf16),
            pltpu.VMEM((ticks - 1, 2, depth, cols_tile), bf16),
            pltpu.VMEM((2, pairs, strip, depth), f32),
            pltpu.VMEM((2, ratio, pairs, thin, depth), f32),
            pltpu.VMEM((2, pairs, thin + TILE, depth), bf16),
            pltpu.VMEM((2, links, pairs, thin + TILE, depth), bf16),
            pltpu.VMEM((2, ratio, nrow, pairs, thin + TILE, depth), bf16),
            pltpu.VMEM((2, pairs, depth, depth), f32),
            pltpu.VMEM((2, pairs, 2, depth, depth), bf16),
            dma((ticks, links)),
            dma((ticks, ncol)),
            dma,
            dma,
            dma((ticks, links, ratio)),
            dma((ticks, nrow)),
            dma((ticks, nrow)),
            dma((ticks, nrow)),
            dma((ticks, nrow)),
            dma((ticks, nrow)),
            dma((ticks, nrow)),
            dma((ticks, links)),
            dma((ticks, nrow)),
            dma((ticks, ratio)),
            dma((ticks, ratio)),
            dma((ticks,)),
            dma((2,)),
            dma((2, ratio)), dma((2, ratio)),
            dma((2, links)), dma((2, links)),
            dma((2, nrow)), dma((2, nrow)),
            dma((2, ratio)), dma((2, ratio)),
        ],
        compiler_params=pltpu.CompilerParams(
            collective_id=0, has_side_effects=True, vmem_limit_bytes=48 * 1024 * 1024
        ),
    )(trailing, v_panels)


def solution(mesh):
    in_specs = (P("row", "col"), P(None, ("row", "col"), None))
    out_specs = (P("row", "col"), P(None, ("row", "col"), None))
    return jax.shard_map(
        on_device, mesh=mesh, in_specs=in_specs, out_specs=out_specs, check_vma=False
    )
```

time: 93.8 us -> 73 us (0.78); the launches traced: 92.3 us -> 72.8 us
  Pallas kernels: 87.7 us -> 68.3 us
    pallas_call x1, Pallas kernels: 87.7 us -> 68.3 us  [on_device(): pl.pallas_call(functools.partial(kernel, nrow, ncol, ratio, scaling), out...]
where the time goes in v2:
time: 73 us; the launch traced here: 72.8 us
  Pallas kernels  68.3 us (94%)
  local copies, waits for them, and re-layouts  3.9 us (5%)
    pallas_call x1, Pallas kernels, on_device(): pl.pallas_call(functools.partial(kernel, nrow, ncol, ratio, scaling), out...  68.3 us
    unnamed x6, local copies, waits for them, and re-layouts  3.9 us

profile of v2, /device:TPU:27, one launch (start us, length us, event | category | flops | bytes accessed | tf_op | source)
XLA Modules:
  0.0 72.8 jit_solution(1142416318337167692)
XLA Ops:
  0.6 0.0 copy-start
  0.6 1.3 %copy-done = f32[768,384]{1,0:T(8,128)S(1)} copy-done((f32[768,384]{1,0:T(8,128)S(1)}, f32[768,384]{1,0:T(8,128)}, u32[]{:S(2)}) %copy-start) | copy-done | bytes 1179672
  1.9 0.0 copy-start.1
  1.9 0.9 %copy-done.1 = bf16[3,96,256]{2,1,0:T(8,128)(2,1)S(1)} copy-done((bf16[3,96,256]{2,1,0:T(8,128)(2,1)S(1)}, bf16[3,96,256]{2,1,0:T(8,128)(2,1)}, u32[]{:S(2)}) %copy-start.1) | copy-done | bytes 147480
  2.8 68.3 %shard_map.41 = (f32[768,384]{1,0:T(8,128)S(1)}, f32[3,96,256]{2,1,0:T(8,128)S(1)}) custom-call(f32[768,384]{1,0:T(8,128)S(1)} %copy-done, bf16[3,96,256]{2,1,0:T(8,128)(2,1)S(1)} %copy-done.1), custom_call_target="tpu_custom_call" | custom-call | tf_op jit(solution)/shard_map/pallas_call | solution.py:504
  71.1 1.0 %copy.6 = f32[768,384]{1,0:T(8,128)} copy(f32[768,384]{1,0:T(8,128)S(1)} %get-tuple-element.4) | data formatting | bytes 2359296
  72.1 0.7 copy.7
Async XLA Ops:
  0.6 1.3 %copy-start = (f32[768,384]{1,0:T(8,128)S(1)}, f32[768,384]{1,0:T(8,128)}, u32[]{:S(2)}) copy-start(f32[768,384]{1,0:T(8,128)} %a_hbm.1) | copy-start | bytes 3538948
  1.9 0.9 %copy-start.1 = (bf16[3,96,256]{2,1,0:T(8,128)(2,1)S(1)}, bf16[3,96,256]{2,1,0:T(8,128)(2,1)}, u32[]{:S(2)}) copy-start(bf16[3,96,256]{2,1,0:T(8,128)(2,1)} %v_ref.1) | copy-start | bytes 442372

commit v3 on v2

--- a/solution.py
+++ b/solution.py
@@ -53,8 +53,8 @@
 def kernel(
     nrow, ncol, ratio, scaling,
     a_hbm, v_ref, out_ref, w_ref,
-    a_ref, ab, vr, vt, vtt, part, sent, got, own, wcc, wrc, wct, wr, zt, gp, ga, gs, gc, gq, gram, fact,
-    v_send, v_recv, vt_send, vt_recv, vx_send, vo_send, vx_recv,
+    a_ref, ab, vo, vr, vt, vtt, part, sent, got, own, wcc, wrc, wct, wr, zt, gp, ga, gs, gc, gq, gram, fact,
+    v_send, v_recv, vt_send, vt_recv, vx_send, vo_send, vx_recv, vs_send, vs_recv, vl_sem,
     rs_send, rs_recv, wc_send, wc_recv, wr_send, wr_recv, wx_send, wx_recv, local_sem, in_sem,
     ga_send, ga_recv, gb_send, gb_recv, gd_send, gd_recv, ge_send, ge_recv,
 ):
@@ -93,6 +93,8 @@
 
     a_in = pltpu.make_async_copy(a_hbm, a_ref, in_sem.at[0])
     v_own = pltpu.make_async_copy(v_ref, vr.at[:, rows(c)], in_sem.at[1])
+    v_src = pltpu.make_async_copy(v_ref, vo, in_sem.at[2])
+    v_src.start()
     v_own.start()
     a_in.start()
     barrier = pltpu.get_barrier_semaphore()
@@ -112,20 +114,27 @@
         greet(from_row, from_col)
         greet(to_row, to_col)
 
+    v_src.wait()
     v_own.wait()
     pl.semaphore_wait(barrier, nrow + ratio + links - 3 + jnp.where(stays, 0, 2))
 
+    def start(copy):
+        copy.start()
+
+    def wait_send(copy):
+        copy.wait_send()
+
     def v_out(t, i):
-        spot = vr.at[t, rows(c)]
-        return remote(
-            spot, spot, v_send.at[t, i], v_recv.at[t, c], r, ((q + i) % links) * ratio + j
+        return remote(
+            vo.at[t], vr.at[t, rows(c)], v_send.at[t, i], v_recv.at[t, c],
+            r, ((q + i) % links) * ratio + j,
         )
 
     def v_side(t, i, k):
         at = ((q + i) % links) * ratio + j
         spot = vr.at[t, rows(at)]
         return remote(
-            spot, spot, vx_send.at[t, i, k - 1], v_recv.at[t, at],
+            spot if i else vo.at[t], spot, vx_send.at[t, i, k - 1], v_recv.at[t, at],
             r, q * ratio + (j + k) % ratio,
         )
 
@@ -133,8 +142,22 @@
         spot = vr.at[t, rows(col)]
         return pltpu.make_async_copy(spot, spot, v_recv.at[t, col])
 
-    vt_move = remote(v_ref, vt.at[:, rows(to_row)], vt_send, vt_recv, to_row, to_col)
-    vt_in = pltpu.make_async_copy(v_ref, vt.at[:, rows(r)], vt_recv)
+    def vt_move(t):
+        return remote(
+            vo.at[t], vt.at[t, rows(to_row)], vt_send.at[t], vt_recv.at[t], to_row, to_col
+        )
+
+    def vt_in(t):
+        return pltpu.make_async_copy(vo.at[t], vt.at[t, rows(r)], vt_recv.at[t])
+
+    def vt_start(t):
+        @pl.when(stays)
+        def _():
+            vt_in(t).start()
+
+        @pl.when(jnp.logical_not(stays))
+        def _():
+            vt_move(t).start()
 
     def vt_out(t, i):
         peer = (r + i) % nrow
@@ -145,7 +168,44 @@
         spot = vt.at[t, rows(peer)]
         return pltpu.make_async_copy(spot, spot, vx_recv.at[t, peer])
 
-    def v_gather(t):
+    source = q == r
+    aside = jnp.logical_not(source)
+
+    def seats(at):
+        return pl.ds(pl.multiple_of(at * cols_tile, cols_tile), cols_tile)
+
+    def vs_out(t, k):
+        return remote(
+            vt.at[t], vr.at[t, seats(j)], vs_send.at[t, k], vs_recv.at[t, j],
+            r, q * ratio + (j + k) % ratio,
+        )
+
+    def vs_in(t, k):
+        at = (j + k) % ratio
+        spot = vr.at[t, seats(at)]
+        return pltpu.make_async_copy(spot, spot, vs_recv.at[t, at])
+
+    def vs_keep(t):
+        return pltpu.make_async_copy(vt.at[t], vr.at[t, seats(j)], vl_sem.at[t])
+
+    def v_each(t, act):
+        for i in range(1, links):
+            if t == 0:
+                act(v_out(t, i))
+            else:
+                @pl.when((q + i) % links != r)
+                def _():
+                    act(v_out(t, i))
+        if t == 0:
+            for k in range(1, ratio):
+                act(v_side(t, 0, k))
+        else:
+            @pl.when(aside)
+            def _():
+                for k in range(1, ratio):
+                    act(v_side(t, 0, k))
+
+    def v_direct(t):
         for i in range(1, links):
             v_in(t, ((q + i) % links) * ratio + j).wait()
             for k in range(1, ratio):
@@ -154,24 +214,55 @@
             for k in range(1, ratio):
                 v_in(t, ((q + i) % links) * ratio + (j + k) % ratio).wait()
 
-    def vt_spread():
+    closed, gathered = set(), set()
+
+    def v_gather(t):
+        if t == 0:
+            v_direct(t)
+            return
+
+        gathered.add(t)
+
+        @pl.when(aside)
+        def _():
+            v_direct(t)
+
+        @pl.when(source)
+        def _():
+            if t not in closed:
+                vt_arrive(t)
+            vs_keep(t).start()
+            for k in range(1, ratio):
+                vs_out(t, k).start()
+            for k in range(1, ratio):
+                vs_in(t, k).wait()
+            vs_keep(t).wait()
+
+    def vt_spread(t):
         @pl.when(stays)
         def _():
-            vt_in.wait()
+            vt_in(t).wait()
 
         @pl.when(jnp.logical_not(stays))
         def _():
-            vt_move.wait()
-
-        for t in range(ticks):
-            for i in range(1, nrow):
-                vt_out(t, i).start()
-
-    def vt_close():
-        for t in range(ticks):
-            for i in range(1, nrow):
-                vt_got(t, (r + i) % nrow).wait()
-            vtt[t] = vt[t].astype(jnp.float32).T.astype(jnp.bfloat16)
+            vt_move(t).wait()
+
+        for i in range(1, nrow):
+            vt_out(t, i).start()
+
+    def vt_arrive(t):
+        for i in range(1, nrow):
+            vt_got(t, (r + i) % nrow).wait()
+
+    def vt_close(t):
+        if t in gathered:
+            @pl.when(aside)
+            def _():
+                vt_arrive(t)
+        else:
+            vt_arrive(t)
+            closed.add(t)
+        vtt[t] = vt[t].astype(jnp.float32).T.astype(jnp.bfloat16)
 
     def rs_out(t, i):
         peer = (r + i) % nrow
@@ -189,8 +280,6 @@
     def wc_in(t, peer):
         spot = wcc.at[t, peer]
         return pltpu.make_async_copy(spot, spot, wc_recv.at[t, peer])
-
-    source = q == r
 
     def wr_out(t, i):
         return remote(
@@ -232,11 +321,13 @@
             total = total + decode(got.at[t, peer], strip)
         total = total * scaling
         encode(wcc.at[t, r], total)
+        own[t, 0], own[t, 1] = halves(total)
+
+    def spread(t):
         for i in range(1, nrow):
             wc_out(t, i).start()
         for i in range(1, links):
             wr_out(t, i).start()
-        own[t, 0], own[t, 1] = halves(total)
 
     def relay(t):
         for i in range(1, nrow):
@@ -391,60 +482,55 @@
         out_ref[...] = out_ref[...] - half * terms
 
 
-    for t in range(ticks):
-        if t == 1:
-            @pl.when(stays)
-            def _():
-                vt_in.start()
-
-            @pl.when(jnp.logical_not(stays))
-            def _():
-                vt_move.start()
-        for i in range(1, links):
-            v_out(t, i).start()
-        for k in range(1, ratio):
-            v_side(t, 0, k).start()
-
+    vt_start(1)
     a_in.wait()
     ab[0], ab[1] = halves(a_ref[...])
-
+    out_ref[...] = a_ref[...]
+    vt_start(2)
+    v_each(1, start)
+    vt_start(0)
+    vt_spread(1)
+    vt_spread(2)
+    v_each(0, start)
+    vt_spread(0)
+    partial(1)
+    v_each(2, start)
     partial(0)
-    vt_spread()
-    partial(1)
+    collect(1)
+    spread(1)
+    vt_close(2)
+    vt_close(1)
     collect(0)
-    vt_close()
+    vt_close(0)
     gram_a(0)
-    collect(1)
+    spread(0)
+    partial(2)
+    gram_b(0)
     gram_a(1)
-    gram_b(0)
     gram_b(1)
-    partial(2)
-    relay(0)
-    open_cols(0)
+    relay(1)
     gram_d(0)
     collect(2)
+    relay(0)
+    spread(2)
+    open_cols(0)
+    open_rows(1)
     gram_d(1)
-    relay(1)
+    open_rows(0)
     open_cols(1)
     gram_e(0)
-    open_rows(0)
-    gram_e(1)
     gram_f(0)
     make_c()
-    make_z()
-    out_ref[...] = a_ref[...]
-    minus(dot2(both(wr.at[0]), both(zt.at[0]), NN))
     relay(2)
     open_cols(2)
-    open_rows(1)
-    minus(dot2(both(wr.at[1]), both(zt.at[1]), NN))
-    one = full(wct.at[1]) + dot2(kept(0, 0), both(wct.at[0]), TN)
-    two = (
+    make_z()
+    gram_e(1)
+    part[1] = full(wct.at[1]) + dot2(kept(0, 0), both(wct.at[0]), TN)
+    part[2] = (
         full(wct.at[2]) + dot2(kept(0, 1), both(wct.at[0]), TN)
         + dot2(kept(0, 2), both(wct.at[1]), TN)
     )
-    part[1] = one
-    part[2] = two
+    open_rows(2)
     gram_f(1)
     make_d()
     zero = full(wct.at[0]) + dot4(kept(1, 0), vtt[1], NN) + dot4(kept(1, 1), vtt[2], NN)
@@ -453,7 +539,6 @@
     minus(dot3(vr[1], halves(one), NN))
     two = part[2] + dot4(kept(1, 1), vtt[0], TN) + dot4(kept(1, 2), vtt[1], TN)
     minus(dot3(vr[2], halves(two), NN))
-    open_rows(2)
     minus(dot4(both(wr.at[2]), vtt[2], NN))
     mine = rows(c)
     for t in range(ticks):
@@ -463,14 +548,26 @@
                 total = total + dot2((wr[u, 0, mine], wr[u, 1, mine]), kept(0, m), NN)
                 total = total + dot3(vr[u, mine], kept(1, m), NN)
         w_ref[t] = total
+    minus(dot2(both(wr.at[1]), both(zt.at[1]), NN))
+    minus(dot2(both(wr.at[0]), both(zt.at[0]), NN))
 
     for t in range(ticks):
+        v_each(t, wait_send)
         for i in range(1, links):
-            v_out(t, i).wait_send()
             wr_out(t, i).wait_send()
         for k in range(1, ratio):
-            for i in range(links):
-                v_side(t, i, k).wait_send()
+            if t == 0:
+                for i in range(1, links):
+                    v_side(t, i, k).wait_send()
+            else:
+                @pl.when(aside)
+                def _():
+                    for i in range(1, links):
+                        v_side(t, i, k).wait_send()
+
+                @pl.when(source)
+                def _():
+                    vs_out(t, k).wait_send()
             wx_out(t, k).wait_send()
         for i in range(1, nrow):
             vt_out(t, i).wait_send()
@@ -512,6 +609,7 @@
         scratch_shapes=[
             pltpu.VMEM((rows_tile, cols_tile), f32),
             pltpu.VMEM((2, rows_tile, cols_tile), bf16),
+            pltpu.VMEM((ticks, piece, depth), bf16),
             pltpu.VMEM((ticks, rows_tile, depth), bf16),
             pltpu.VMEM((ticks, cols_tile, depth), bf16),
             pltpu.VMEM((ticks, depth, cols_tile), bf16),
@@ -533,11 +631,14 @@
             pltpu.VMEM((2, pairs, 2, depth, depth), bf16),
             dma((ticks, links)),
             dma((ticks, ncol)),
-            dma,
-            dma,
+            dma((ticks,)),
+            dma((ticks,)),
             dma((ticks, links, ratio)),
             dma((ticks, nrow)),
             dma((ticks, nrow)),
+            dma((ticks, ratio)),
+            dma((ticks, ratio)),
+            dma((ticks,)),
             dma((ticks, nrow)),
             dma((ticks, nrow)),
             dma((ticks, nrow)),
@@ -547,7 +648,7 @@
             dma((ticks, ratio)),
             dma((ticks, ratio)),
             dma((ticks,)),
-            dma((2,)),
+            dma((3,)),
             dma((2, ratio)), dma((2, ratio)),
             dma((2, links)), dma((2, links)),
             dma((2, nrow)), dma((2, nrow)),

time: 73 us -> 67.6 us (0.926)
  Pallas kernels: 68.3 us -> 62.8 us
    pallas_call x1, Pallas kernels: 68.3 us -> 62.8 us  [on_device(): pl.pallas_call(functools.partial(kernel, nrow, ncol, ratio, scaling), out...]
where the time goes in v3:
time: 67.6 us; the launch traced here: 67.4 us
  Pallas kernels  62.8 us (93%)
  local copies, waits for them, and re-layouts  3.9 us (6%)
    pallas_call x1, Pallas kernels, on_device(): pl.pallas_call(functools.partial(kernel, nrow, ncol, ratio, scaling), out...  62.8 us
    unnamed x6, local copies, waits for them, and re-layouts  3.9 us

profile of v3, /device:TPU:27, one launch (start us, length us, event | category | flops | bytes accessed | tf_op | source)
XLA Modules:
  0.0 67.4 jit_solution(15599377678634218110)
XLA Ops:
  0.6 0.0 copy-start
  0.6 1.3 %copy-done = f32[768,384]{1,0:T(8,128)S(1)} copy-done((f32[768,384]{1,0:T(8,128)S(1)}, f32[768,384]{1,0:T(8,128)}, u32[]{:S(2)}) %copy-start) | copy-done | bytes 1179672
  1.9 0.0 copy-start.1
  1.9 0.9 %copy-done.1 = bf16[3,96,256]{2,1,0:T(8,128)(2,1)S(1)} copy-done((bf16[3,96,256]{2,1,0:T(8,128)(2,1)S(1)}, bf16[3,96,256]{2,1,0:T(8,128)(2,1)}, u32[]{:S(2)}) %copy-start.1) | copy-done | bytes 147480
  2.8 62.8 %shard_map.41 = (f32[768,384]{1,0:T(8,128)S(1)}, f32[3,96,256]{2,1,0:T(8,128)S(1)}) custom-call(f32[768,384]{1,0:T(8,128)S(1)} %copy-done, bf16[3,96,256]{2,1,0:T(8,128)(2,1)S(1)} %copy-done.1), custom_call_target="tpu_custom_call" | custom-call | tf_op jit(solution)/shard_map/pallas_call | solution.py:601
  65.7 1.0 %copy.6 = f32[768,384]{1,0:T(8,128)} copy(f32[768,384]{1,0:T(8,128)S(1)} %get-tuple-element.4) | data formatting | bytes 2359296
  66.7 0.7 %copy.7 = f32[3,96,256]{2,1,0:T(8,128)} copy(f32[3,96,256]{2,1,0:T(8,128)S(1)} %get-tuple-element.5) | data formatting | bytes 589824
Async XLA Ops:
  0.6 1.3 %copy-start = (f32[768,384]{1,0:T(8,128)S(1)}, f32[768,384]{1,0:T(8,128)}, u32[]{:S(2)}) copy-start(f32[768,384]{1,0:T(8,128)} %a_hbm.1) | copy-start | bytes 3538948
  1.9 0.9 %copy-start.1 = (bf16[3,96,256]{2,1,0:T(8,128)(2,1)S(1)}, bf16[3,96,256]{2,1,0:T(8,128)(2,1)}, u32[]{:S(2)}) copy-start(bf16[3,96,256]{2,1,0:T(8,128)(2,1)} %v_ref.1) | copy-start | bytes 442372

commit v4 on v3

--- a/solution.py
+++ b/solution.py
@@ -45,15 +45,27 @@
     ref[pl.ds(ref.shape[0] - TILE, TILE)] = jnp.broadcast_to(peak, (TILE, x.shape[1]))
 
 
-def decode(ref, rows):
+def encode_all(ref, parts):
+    rows = parts[0].shape[0]
+    peak = jnp.max(jnp.abs(parts[0]), axis=0, keepdims=True)
+    for x in parts[1:]:
+        peak = jnp.maximum(peak, jnp.max(jnp.abs(x), axis=0, keepdims=True))
+    peak = jnp.maximum(peak, TINY).astype(jnp.bfloat16)
+    scale = SPAN / peak.astype(jnp.float32)
+    for i, x in enumerate(parts):
+        ref[pl.ds(i * rows, rows)] = jnp.exp2(x * scale).astype(jnp.bfloat16)
+    ref[pl.ds(ref.shape[0] - TILE, TILE)] = jnp.broadcast_to(peak, (TILE, peak.shape[1]))
+
+
+def decode(ref, rows, at=0):
     peak = ref[pl.ds(ref.shape[0] - TILE, TILE)].astype(jnp.float32)[:1]
-    return jnp.log2(ref[pl.ds(0, rows)].astype(jnp.float32)) * (peak * (1.0 / SPAN))
+    return jnp.log2(ref[pl.ds(at, rows)].astype(jnp.float32)) * (peak * (1.0 / SPAN))
 
 
 def kernel(
     nrow, ncol, ratio, scaling,
     a_hbm, v_ref, out_ref, w_ref,
-    a_ref, ab, vo, vr, vt, vtt, part, sent, got, own, wcc, wrc, wct, wr, zt, gp, ga, gs, gc, gq, gram, fact,
+    a_ref, ab, vo, vr, vt, vtt, part, sent, got, own, wcc, wrc, wct, wr, zt, gp, gt, ga, gs, gc, gq, gram, fact,
     v_send, v_recv, vt_send, vt_recv, vx_send, vo_send, vx_recv, vs_send, vs_recv, vl_sem,
     rs_send, rs_recv, wc_send, wc_recv, wr_send, wr_recv, wx_send, wx_recv, local_sem, in_sem,
     ga_send, ga_recv, gb_send, gb_recv, gd_send, gd_recv, ge_send, ge_recv,
@@ -71,6 +83,7 @@
     fix = scaling * half
     strip = depth // nrow
     thin = strip // ratio
+    steps = gs.shape[1]
 
     def rows(at):
         return pl.ds(pl.multiple_of(at * piece, piece), piece)
@@ -371,14 +384,14 @@
         return pltpu.make_async_copy(ga.at[k, at], ga.at[k, at], ga_recv.at[k, at])
 
     def gb_out(k, s):
-        return remote(
-            gs.at[k], gc.at[k, q], gb_send.at[k, s], gb_recv.at[k, q],
-            r, ((q + s) % links) * ratio + j,
+        far = 2**s
+        to = q + far - 2 * far * ((q // far) % 2)
+        return remote(
+            gs.at[k, s], gc.at[k, s], gb_send.at[k, s], gb_recv.at[k, s], r, to * ratio + j
         )
 
     def gb_in(k, s):
-        at = (q + s) % links
-        return pltpu.make_async_copy(gc.at[k, at], gc.at[k, at], gb_recv.at[k, at])
+        return pltpu.make_async_copy(gc.at[k, s], gc.at[k, s], gb_recv.at[k, s])
 
     def gd_out(k, i):
         spot = gq.at[k, j, r]
@@ -409,23 +422,32 @@
     def gram_b(k):
         for s in range(1, ratio):
             ga_in(k, s).wait()
+        totals = []
         for m in range(pairs):
             total = gp[k, m, thins(j)]
             for s in range(1, ratio):
                 total = total + ga[k, (j + s) % ratio, m]
-            gp[k, m, thins(j)] = total
-            encode(gs.at[k, m], total)
-        for s in range(1, links):
+            gt[k, m] = total
+            totals.append(total)
+        encode_all(gs.at[k, 0], totals)
+        gb_out(k, 0).start()
+
+    def gram_add(k, s):
+        gb_in(k, s).wait()
+        totals = []
+        for m in range(pairs):
+            total = gt[k, m] + decode(gc.at[k, s], thin, m * thin)
+            gt[k, m] = total
+            totals.append(total)
+        return totals
+
+    def gram_c(k):
+        for s in range(1, steps):
+            encode_all(gs.at[k, s], gram_add(k, s - 1))
             gb_out(k, s).start()
 
     def gram_d(k):
-        for s in range(1, links):
-            gb_in(k, s).wait()
-        for m in range(pairs):
-            total = gp[k, m, thins(j)]
-            for s in range(1, links):
-                total = total + decode(gc.at[k, (q + s) % links, m], thin)
-            encode(gq.at[k, j, r, m], total)
+        encode_all(gq.at[k, j, r], gram_add(k, steps - 1))
         for i in range(1, nrow):
             gd_out(k, i).start()
 
@@ -442,7 +464,7 @@
             for i in range(nrow):
                 for s in range(ratio):
                     at = pl.ds(i * strip + s * thin, thin)
-                    gram[k, m, at] = decode(gq.at[k, s, i, m], thin)
+                    gram[k, m, at] = decode(gq.at[k, s, i], thin, m * thin)
 
     def keep(k, m, x):
         fact[k, m, 0], fact[k, m, 1] = halves(x)
@@ -483,54 +505,58 @@
 
 
     vt_start(1)
+    vt_start(2)
     a_in.wait()
     ab[0], ab[1] = halves(a_ref[...])
     out_ref[...] = a_ref[...]
-    vt_start(2)
     v_each(1, start)
     vt_start(0)
     vt_spread(1)
+    v_each(0, start)
     vt_spread(2)
-    v_each(0, start)
     vt_spread(0)
     partial(1)
     v_each(2, start)
     partial(0)
+    vt_close(2)
+    vt_close(1)
+    vt_close(0)
+    gram_a(0)
     collect(1)
     spread(1)
-    vt_close(2)
-    vt_close(1)
+    gram_b(0)
     collect(0)
-    vt_close(0)
-    gram_a(0)
     spread(0)
-    partial(2)
-    gram_b(0)
+    gram_c(0)
     gram_a(1)
     gram_b(1)
+    partial(2)
+    gram_d(0)
+    relay(0)
     relay(1)
-    gram_d(0)
+    gram_c(1)
     collect(2)
-    relay(0)
+    open_rows(0)
     spread(2)
-    open_cols(0)
+    gram_d(1)
     open_rows(1)
-    gram_d(1)
-    open_rows(0)
-    open_cols(1)
     gram_e(0)
     gram_f(0)
     make_c()
+    open_cols(1)
+    make_z()
     relay(2)
+    open_cols(0)
+    minus(dot2(both(wr.at[0]), both(zt.at[0]), NN))
+    open_rows(2)
     open_cols(2)
-    make_z()
     gram_e(1)
+    minus(dot2(both(wr.at[1]), both(zt.at[1]), NN))
     part[1] = full(wct.at[1]) + dot2(kept(0, 0), both(wct.at[0]), TN)
     part[2] = (
         full(wct.at[2]) + dot2(kept(0, 1), both(wct.at[0]), TN)
         + dot2(kept(0, 2), both(wct.at[1]), TN)
     )
-    open_rows(2)
     gram_f(1)
     make_d()
     zero = full(wct.at[0]) + dot4(kept(1, 0), vtt[1], NN) + dot4(kept(1, 1), vtt[2], NN)
@@ -548,8 +574,6 @@
                 total = total + dot2((wr[u, 0, mine], wr[u, 1, mine]), kept(0, m), NN)
                 total = total + dot3(vr[u, mine], kept(1, m), NN)
         w_ref[t] = total
-    minus(dot2(both(wr.at[1]), both(zt.at[1]), NN))
-    minus(dot2(both(wr.at[0]), both(zt.at[0]), NN))
 
     for t in range(ticks):
         v_each(t, wait_send)
@@ -578,7 +602,7 @@
         for s in range(1, ratio):
             ga_out(k, s).wait_send()
             ge_out(k, s).wait_send()
-        for s in range(1, links):
+        for s in range(steps):
             gb_out(k, s).wait_send()
         for i in range(1, nrow):
             gd_out(k, i).wait_send()
@@ -595,6 +619,7 @@
     pairs = ticks * (ticks - 1) // 2
     strip = depth // nrow
     thin = strip // ratio
+    steps = links.bit_length() - 1
     dma = pltpu.SemaphoreType.DMA
     vmem = pl.BlockSpec(memory_space=pltpu.VMEM)
     f32, bf16 = jnp.float32, jnp.bfloat16
@@ -623,10 +648,11 @@
             pltpu.VMEM((ticks, 2, rows_tile, depth), bf16),
             pltpu.VMEM((ticks - 1, 2, depth, cols_tile), bf16),
             pltpu.VMEM((2, pairs, strip, depth), f32),
+            pltpu.VMEM((2, pairs, thin, depth), f32),
             pltpu.VMEM((2, ratio, pairs, thin, depth), f32),
-            pltpu.VMEM((2, pairs, thin + TILE, depth), bf16),
-            pltpu.VMEM((2, links, pairs, thin + TILE, depth), bf16),
-            pltpu.VMEM((2, ratio, nrow, pairs, thin + TILE, depth), bf16),
+            pltpu.VMEM((2, steps, pairs * thin + TILE, depth), bf16),
+            pltpu.VMEM((2, steps, pairs * thin + TILE, depth), bf16),
+            pltpu.VMEM((2, ratio, nrow, pairs * thin + TILE, depth), bf16),
             pltpu.VMEM((2, pairs, depth, depth), f32),
             pltpu.VMEM((2, pairs, 2, depth, depth), bf16),
             dma((ticks, links)),
@@ -650,7 +676,7 @@
             dma((ticks,)),
             dma((3,)),
             dma((2, ratio)), dma((2, ratio)),
-            dma((2, links)), dma((2, links)),
+            dma((2, steps)), dma((2, steps)),
             dma((2, nrow)), dma((2, nrow)),
             dma((2, ratio)), dma((2, ratio)),
         ],

time: 67.6 us -> 62.3 us (0.922)
  the two profiles are of different devices: /device:TPU:27 before, /device:TPU:0 now
where the time goes in v4:
time: 62.3 us; the launch traced here: 62.2 us
  Pallas kernels  57.6 us (92%)
  local copies, waits for them, and re-layouts  3.9 us (6%)
  between operations  0.65 us (1%)
    pallas_call x1, Pallas kernels, on_device(): pl.pallas_call(functools.partial(kernel, nrow, ncol, ratio, scaling), out...  57.6 us
    unnamed x6, local copies, waits for them, and re-layouts  3.9 us

profile of v4, /device:TPU:0, one launch (start us, length us, event | category | flops | bytes accessed | tf_op | source)
XLA Modules:
  0.0 62.2 jit_solution(2459949120236856725)
XLA Ops:
  0.6 0.0 copy-start
  0.6 1.3 %copy-done = f32[768,384]{1,0:T(8,128)S(1)} copy-done((f32[768,384]{1,0:T(8,128)S(1)}, f32[768,384]{1,0:T(8,128)}, u32[]{:S(2)}) %copy-start) | copy-done | bytes 1179672
  1.9 0.0 copy-start.1
  1.9 0.9 %copy-done.1 = bf16[3,96,256]{2,1,0:T(8,128)(2,1)S(1)} copy-done((bf16[3,96,256]{2,1,0:T(8,128)(2,1)S(1)}, bf16[3,96,256]{2,1,0:T(8,128)(2,1)}, u32[]{:S(2)}) %copy-start.1) | copy-done | bytes 147480
  2.8 57.6 %shard_map.41 = (f32[768,384]{1,0:T(8,128)S(1)}, f32[3,96,256]{2,1,0:T(8,128)S(1)}) custom-call(f32[768,384]{1,0:T(8,128)S(1)} %copy-done, bf16[3,96,256]{2,1,0:T(8,128)(2,1)S(1)} %copy-done.1), custom_call_target="tpu_custom_call" | custom-call | tf_op jit(solution)/shard_map/pallas_call | solution.py:626
  60.4 1.0 %copy.6 = f32[768,384]{1,0:T(8,128)} copy(f32[768,384]{1,0:T(8,128)S(1)} %get-tuple-element.4) | data formatting | bytes 2359296
  61.5 0.7 %copy.7 = f32[3,96,256]{2,1,0:T(8,128)} copy(f32[3,96,256]{2,1,0:T(8,128)S(1)} %get-tuple-element.5) | data formatting | bytes 589824
Async XLA Ops:
  0.6 1.3 %copy-start = (f32[768,384]{1,0:T(8,128)S(1)}, f32[768,384]{1,0:T(8,128)}, u32[]{:S(2)}) copy-start(f32[768,384]{1,0:T(8,128)} %a_hbm.1) | copy-start | bytes 3538948
  1.9 0.9 %copy-start.1 = (bf16[3,96,256]{2,1,0:T(8,128)(2,1)S(1)}, bf16[3,96,256]{2,1,0:T(8,128)(2,1)}, u32[]{:S(2)}) copy-start(bf16[3,96,256]{2,1,0:T(8,128)(2,1)} %v_ref.1) | copy-start | bytes 442372

commit v5 on v4

--- a/solution.py
+++ b/solution.py
@@ -15,6 +15,7 @@
 SPAN = 124.0
 TINY = 1e-30
 TILE = 8
+DIRECT = ()
 
 
 def dot(a, b, dims):
@@ -36,6 +37,15 @@
 
 def dot4(a, b, dims):
     return dot(a[0], b, dims) + dot(a[1], b, dims)
+
+
+def fold(x):
+    width = x.shape[1] // 2
+    return x[:, :width] + x[:, width:]
+
+
+def wide(pair):
+    return jnp.concatenate(pair, axis=1)
 
 
 def encode(ref, x):
@@ -203,13 +213,13 @@
 
     def v_each(t, act):
         for i in range(1, links):
-            if t == 0:
+            if t in DIRECT:
                 act(v_out(t, i))
             else:
                 @pl.when((q + i) % links != r)
                 def _():
                     act(v_out(t, i))
-        if t == 0:
+        if t in DIRECT:
             for k in range(1, ratio):
                 act(v_side(t, 0, k))
         else:
@@ -230,7 +240,7 @@
     closed, gathered = set(), set()
 
     def v_gather(t):
-        if t == 0:
+        if t in DIRECT:
             v_direct(t)
             return
 
@@ -320,7 +330,7 @@
 
     def partial(t):
         v_gather(t)
-        part[t] = dot(vr[t], ab[0], TN) + dot(vr[t], ab[1], TN)
+        part[t] = fold(dot(vr[t], ab[...], TN))
         for i in range(1, nrow):
             peer = (r + i) % nrow
             encode(sent.at[t, peer], part[t, strips(peer)])
@@ -466,6 +476,10 @@
                     at = pl.ds(i * strip + s * thin, thin)
                     gram[k, m, at] = decode(gq.at[k, s, i], thin, m * thin)
 
+    def times(k, m, x):
+        y = dot(fact[k, m].reshape(2 * depth, depth), x, NN)
+        return y[:depth] + y[depth:]
+
     def keep(k, m, x):
         fact[k, m, 0], fact[k, m, 1] = halves(x)
 
@@ -496,9 +510,9 @@
     def make_z():
         zt[0, 0], zt[0, 1] = halves(
             vtt[0].astype(jnp.float32)
-            + dot4(kept(0, 0), vtt[1], NN) + dot4(kept(0, 1), vtt[2], NN)
-        )
-        zt[1, 0], zt[1, 1] = halves(vtt[1].astype(jnp.float32) + dot4(kept(0, 2), vtt[2], NN))
+            + times(0, 0, vtt[1]) + times(0, 1, vtt[2])
+        )
+        zt[1, 0], zt[1, 1] = halves(vtt[1].astype(jnp.float32) + times(0, 2, vtt[2]))
 
     def minus(terms):
         out_ref[...] = out_ref[...] - half * terms
@@ -507,64 +521,64 @@
     vt_start(1)
     vt_start(2)
     a_in.wait()
-    ab[0], ab[1] = halves(a_ref[...])
+    ab[...] = wide(halves(a_ref[...]))
     out_ref[...] = a_ref[...]
+    vt_start(0)
     v_each(1, start)
-    vt_start(0)
+    v_each(2, start)
     vt_spread(1)
-    v_each(0, start)
     vt_spread(2)
     vt_spread(0)
+    v_each(0, start)
     partial(1)
-    v_each(2, start)
+    vt_close(1)
+    partial(2)
     partial(0)
+    vt_close(0)
     vt_close(2)
-    vt_close(1)
-    vt_close(0)
     gram_a(0)
+    gram_b(0)
     collect(1)
     spread(1)
-    gram_b(0)
     collect(0)
+    gram_a(1)
+    gram_c(0)
+    gram_b(1)
+    collect(2)
     spread(0)
-    gram_c(0)
-    gram_a(1)
-    gram_b(1)
-    partial(2)
+    gram_c(1)
+    relay(1)
     gram_d(0)
+    open_rows(1)
+    spread(2)
     relay(0)
-    relay(1)
-    gram_c(1)
-    collect(2)
-    open_rows(0)
-    spread(2)
     gram_d(1)
-    open_rows(1)
     gram_e(0)
     gram_f(0)
     make_c()
-    open_cols(1)
+    open_rows(0)
     make_z()
     relay(2)
+    open_cols(1)
+    open_cols(2)
     open_cols(0)
-    minus(dot2(both(wr.at[0]), both(zt.at[0]), NN))
-    open_rows(2)
-    open_cols(2)
-    gram_e(1)
-    minus(dot2(both(wr.at[1]), both(zt.at[1]), NN))
+    minus(fold(dot(wr[1, 0], wide(both(zt.at[1])), NN)) + dot(wr[1, 1], zt[1, 0], NN))
     part[1] = full(wct.at[1]) + dot2(kept(0, 0), both(wct.at[0]), TN)
     part[2] = (
         full(wct.at[2]) + dot2(kept(0, 1), both(wct.at[0]), TN)
         + dot2(kept(0, 2), both(wct.at[1]), TN)
     )
+    gram_e(1)
+    open_rows(2)
+    minus(fold(dot(wr[0, 0], wide(both(zt.at[0])), NN)) + dot(wr[0, 1], zt[0, 0], NN))
     gram_f(1)
     make_d()
-    zero = full(wct.at[0]) + dot4(kept(1, 0), vtt[1], NN) + dot4(kept(1, 1), vtt[2], NN)
-    minus(dot3(vr[0], halves(zero), NN))
-    one = part[1] + dot4(kept(1, 0), vtt[0], TN) + dot4(kept(1, 2), vtt[2], NN)
-    minus(dot3(vr[1], halves(one), NN))
+    zero = full(wct.at[0]) + times(1, 0, vtt[1]) + times(1, 1, vtt[2])
+    minus(fold(dot(vr[0], wide(halves(zero)), NN)))
+    one = part[1] + dot4(kept(1, 0), vtt[0], TN) + times(1, 2, vtt[2])
+    minus(fold(dot(vr[1], wide(halves(one)), NN)))
     two = part[2] + dot4(kept(1, 1), vtt[0], TN) + dot4(kept(1, 2), vtt[1], TN)
-    minus(dot3(vr[2], halves(two), NN))
+    minus(fold(dot(vr[2], wide(halves(two)), NN)))
     minus(dot4(both(wr.at[2]), vtt[2], NN))
     mine = rows(c)
     for t in range(ticks):
@@ -580,7 +594,7 @@
         for i in range(1, links):
             wr_out(t, i).wait_send()
         for k in range(1, ratio):
-            if t == 0:
+            if t in DIRECT:
                 for i in range(1, links):
                     v_side(t, i, k).wait_send()
             else:
@@ -633,7 +647,7 @@
         out_specs=(vmem, vmem),
         scratch_shapes=[
             pltpu.VMEM((rows_tile, cols_tile), f32),
-            pltpu.VMEM((2, rows_tile, cols_tile), bf16),
+            pltpu.VMEM((rows_tile, 2 * cols_tile), bf16),
             pltpu.VMEM((ticks, piece, depth), bf16),
             pltpu.VMEM((ticks, rows_tile, depth), bf16),
             pltpu.VMEM((ticks, cols_tile, depth), bf16),

time: 62.3 us -> 60.5 us (0.971)
  the two profiles are of different devices: /device:TPU:0 before, /device:TPU:27 now
where the time goes in v5:
time: 60.5 us; the launch traced here: 59.3 us
  Pallas kernels  54.7 us (90%)
  local copies, waits for them, and re-layouts  3.9 us (6%)
  between operations  0.65 us (1%)
    pallas_call x1, Pallas kernels, on_device(): pl.pallas_call(functools.partial(kernel, nrow, ncol, ratio, scaling), out...  54.7 us
    unnamed x6, local copies, waits for them, and re-layouts  3.9 us

profile of v5, /device:TPU:27, one launch (start us, length us, event | category | flops | bytes accessed | tf_op | source)
XLA Modules:
  0.0 59.3 jit_solution(11114873155016344566)
XLA Ops:
  0.6 0.0 copy-start
  0.6 1.3 %copy-done = f32[768,384]{1,0:T(8,128)S(1)} copy-done((f32[768,384]{1,0:T(8,128)S(1)}, f32[768,384]{1,0:T(8,128)}, u32[]{:S(2)}) %copy-start) | copy-done | bytes 1179672
  1.9 0.0 copy-start.1
  1.9 0.9 %copy-done.1 = bf16[3,96,256]{2,1,0:T(8,128)(2,1)S(1)} copy-done((bf16[3,96,256]{2,1,0:T(8,128)(2,1)S(1)}, bf16[3,96,256]{2,1,0:T(8,128)(2,1)}, u32[]{:S(2)}) %copy-start.1) | copy-done | bytes 147480
  2.8 54.7 %shard_map.41 = (f32[768,384]{1,0:T(8,128)S(1)}, f32[3,96,256]{2,1,0:T(8,128)S(1)}) custom-call(f32[768,384]{1,0:T(8,128)S(1)} %copy-done, bf16[3,96,256]{2,1,0:T(8,128)(2,1)S(1)} %copy-done.1), custom_call_target="tpu_custom_call" | custom-call | tf_op jit(solution)/shard_map/pallas_call | solution.py:640
  57.6 1.0 %copy.6 = f32[768,384]{1,0:T(8,128)} copy(f32[768,384]{1,0:T(8,128)S(1)} %get-tuple-element.4) | data formatting | bytes 2359296
  58.6 0.7 %copy.7 = f32[3,96,256]{2,1,0:T(8,128)} copy(f32[3,96,256]{2,1,0:T(8,128)S(1)} %get-tuple-element.5) | data formatting | bytes 589824
Async XLA Ops:
  0.6 1.3 %copy-start = (f32[768,384]{1,0:T(8,128)S(1)}, f32[768,384]{1,0:T(8,128)}, u32[]{:S(2)}) copy-start(f32[768,384]{1,0:T(8,128)} %a_hbm.1) | copy-start | bytes 3538948
  1.9 0.9 %copy-start.1 = (bf16[3,96,256]{2,1,0:T(8,128)(2,1)S(1)}, bf16[3,96,256]{2,1,0:T(8,128)(2,1)}, u32[]{:S(2)}) copy-start(bf16[3,96,256]{2,1,0:T(8,128)(2,1)} %v_ref.1) | copy-start | bytes 442372

commit v6 on v5

--- a/solution.py
+++ b/solution.py
@@ -571,6 +571,36 @@
     gram_e(1)
     open_rows(2)
     minus(fold(dot(wr[0, 0], wide(both(zt.at[0])), NN)) + dot(wr[0, 1], zt[0, 0], NN))
+    for t in range(ticks):
+        v_each(t, wait_send)
+        for i in range(1, links):
+            wr_out(t, i).wait_send()
+        for k in range(1, ratio):
+            if t in DIRECT:
+                for i in range(1, links):
+                    v_side(t, i, k).wait_send()
+            else:
+                @pl.when(aside)
+                def _():
+                    for i in range(1, links):
+                        v_side(t, i, k).wait_send()
+
+                @pl.when(source)
+                def _():
+                    vs_out(t, k).wait_send()
+        for i in range(1, nrow):
+            vt_out(t, i).wait_send()
+            rs_out(t, i).wait_send()
+            wc_out(t, i).wait_send()
+
+    for k in range(2):
+        for s in range(1, ratio):
+            ga_out(k, s).wait_send()
+        for s in range(steps):
+            gb_out(k, s).wait_send()
+        for i in range(1, nrow):
+            gd_out(k, i).wait_send()
+
     gram_f(1)
     make_d()
     zero = full(wct.at[0]) + times(1, 0, vtt[1]) + times(1, 1, vtt[2])
@@ -590,36 +620,11 @@
         w_ref[t] = total
 
     for t in range(ticks):
-        v_each(t, wait_send)
-        for i in range(1, links):
-            wr_out(t, i).wait_send()
         for k in range(1, ratio):
-            if t in DIRECT:
-                for i in range(1, links):
-                    v_side(t, i, k).wait_send()
-            else:
-                @pl.when(aside)
-                def _():
-                    for i in range(1, links):
-                        v_side(t, i, k).wait_send()
-
-                @pl.when(source)
-                def _():
-                    vs_out(t, k).wait_send()
             wx_out(t, k).wait_send()
-        for i in range(1, nrow):
-            vt_out(t, i).wait_send()
-            rs_out(t, i).wait_send()
-            wc_out(t, i).wait_send()
-
     for k in range(2):
         for s in range(1, ratio):
-            ga_out(k, s).wait_send()
             ge_out(k, s).wait_send()
-        for s in range(steps):
-            gb_out(k, s).wait_send()
-        for i in range(1, nrow):
-            gd_out(k, i).wait_send()
 
 
 def on_device(trailing, v_panels):

time: 60.5 us -> 60.4 us (level)
  no operation moved by 1% of the time
where the time goes in v6:
time: 60.4 us; the launch traced here: 59.2 us
  Pallas kernels  54.6 us (90%)
  local copies, waits for them, and re-layouts  3.9 us (6%)
  between operations  0.65 us (1%)
    pallas_call x1, Pallas kernels, on_device(): pl.pallas_call(functools.partial(kernel, nrow, ncol, ratio, scaling), out...  54.6 us
    unnamed x6, local copies, waits for them, and re-layouts  3.9 us

profile of v6, /device:TPU:27, one launch (start us, length us, event | category | flops | bytes accessed | tf_op | source)
XLA Modules:
  0.0 59.2 jit_solution(12561341108520060758)
XLA Ops:
  0.6 0.0 copy-start
  0.6 1.3 %copy-done = f32[768,384]{1,0:T(8,128)S(1)} copy-done((f32[768,384]{1,0:T(8,128)S(1)}, f32[768,384]{1,0:T(8,128)}, u32[]{:S(2)}) %copy-start) | copy-done | bytes 1179672
  1.9 0.0 copy-start.1
  1.9 0.9 %copy-done.1 = bf16[3,96,256]{2,1,0:T(8,128)(2,1)S(1)} copy-done((bf16[3,96,256]{2,1,0:T(8,128)(2,1)S(1)}, bf16[3,96,256]{2,1,0:T(8,128)(2,1)}, u32[]{:S(2)}) %copy-start.1) | copy-done | bytes 147480
  2.8 54.6 %shard_map.41 = (f32[768,384]{1,0:T(8,128)S(1)}, f32[3,96,256]{2,1,0:T(8,128)S(1)}) custom-call(f32[768,384]{1,0:T(8,128)S(1)} %copy-done, bf16[3,96,256]{2,1,0:T(8,128)(2,1)S(1)} %copy-done.1), custom_call_target="tpu_custom_call" | custom-call | tf_op jit(solution)/shard_map/pallas_call | solution.py:645
  57.5 1.0 %copy.6 = f32[768,384]{1,0:T(8,128)} copy(f32[768,384]{1,0:T(8,128)S(1)} %get-tuple-element.4) | data formatting | bytes 2359296
  58.5 0.7 %copy.7 = f32[3,96,256]{2,1,0:T(8,128)} copy(f32[3,96,256]{2,1,0:T(8,128)S(1)} %get-tuple-element.5) | data formatting | bytes 589824
Async XLA Ops:
  0.6 1.3 %copy-start = (f32[768,384]{1,0:T(8,128)S(1)}, f32[768,384]{1,0:T(8,128)}, u32[]{:S(2)}) copy-start(f32[768,384]{1,0:T(8,128)} %a_hbm.1) | copy-start | bytes 3538948
  1.9 0.9 %copy-start.1 = (bf16[3,96,256]{2,1,0:T(8,128)(2,1)S(1)}, bf16[3,96,256]{2,1,0:T(8,128)(2,1)}, u32[]{:S(2)}) copy-start(bf16[3,96,256]{2,1,0:T(8,128)(2,1)} %v_ref.1) | copy-start | bytes 442372

commit v7 on v6

--- a/solution.py
+++ b/solution.py
@@ -601,6 +601,7 @@
         for i in range(1, nrow):
             gd_out(k, i).wait_send()
 
+    minus(dot4(both(wr.at[2]), vtt[2], NN))
     gram_f(1)
     make_d()
     zero = full(wct.at[0]) + times(1, 0, vtt[1]) + times(1, 1, vtt[2])
@@ -609,7 +610,6 @@
     minus(fold(dot(vr[1], wide(halves(one)), NN)))
     two = part[2] + dot4(kept(1, 1), vtt[0], TN) + dot4(kept(1, 2), vtt[1], TN)
     minus(fold(dot(vr[2], wide(halves(two)), NN)))
-    minus(dot4(both(wr.at[2]), vtt[2], NN))
     mine = rows(c)
     for t in range(ticks):
         total = wr[t, 0, mine].astype(jnp.float32) + wr[t, 1, mine].astype(jnp.float32)

time: 60.4 us -> 60.3 us (level)
  the two profiles are of different devices: /device:TPU:27 before, /device:TPU:0 now
where the time goes in v7:
time: 60.3 us; the launch traced here: 60.1 us
  Pallas kernels  55.6 us (92%)
  local copies, waits for them, and re-layouts  3.9 us (6%)
  between operations  0.65 us (1%)
    pallas_call x1, Pallas kernels, on_device(): pl.pallas_call(functools.partial(kernel, nrow, ncol, ratio, scaling), out...  55.6 us
    unnamed x6, local copies, waits for them, and re-layouts  3.9 us

profile of v7, /device:TPU:0, one launch (start us, length us, event | category | flops | bytes accessed | tf_op | source)
XLA Modules:
  0.0 60.1 jit_solution(5554650638377746218)
XLA Ops:
  0.6 0.0 copy-start
  0.6 1.3 %copy-done = f32[768,384]{1,0:T(8,128)S(1)} copy-done((f32[768,384]{1,0:T(8,128)S(1)}, f32[768,384]{1,0:T(8,128)}, u32[]{:S(2)}) %copy-start) | copy-done | bytes 1179672
  1.9 0.0 copy-start.1
  1.9 0.9 %copy-done.1 = bf16[3,96,256]{2,1,0:T(8,128)(2,1)S(1)} copy-done((bf16[3,96,256]{2,1,0:T(8,128)(2,1)S(1)}, bf16[3,96,256]{2,1,0:T(8,128)(2,1)}, u32[]{:S(2)}) %copy-start.1) | copy-done | bytes 147480
  2.8 55.6 %shard_map.41 = (f32[768,384]{1,0:T(8,128)S(1)}, f32[3,96,256]{2,1,0:T(8,128)S(1)}) custom-call(f32[768,384]{1,0:T(8,128)S(1)} %copy-done, bf16[3,96,256]{2,1,0:T(8,128)(2,1)S(1)} %copy-done.1), custom_call_target="tpu_custom_call" | custom-call | tf_op jit(solution)/shard_map/pallas_call | solution.py:645
  58.4 1.0 %copy.6 = f32[768,384]{1,0:T(8,128)} copy(f32[768,384]{1,0:T(8,128)S(1)} %get-tuple-element.4) | data formatting | bytes 2359296
  59.4 0.7 %copy.7 = f32[3,96,256]{2,1,0:T(8,128)} copy(f32[3,96,256]{2,1,0:T(8,128)S(1)} %get-tuple-element.5) | data formatting | bytes 589824
Async XLA Ops:
  0.6 1.3 %copy-start = (f32[768,384]{1,0:T(8,128)S(1)}, f32[768,384]{1,0:T(8,128)}, u32[]{:S(2)}) copy-start(f32[768,384]{1,0:T(8,128)} %a_hbm.1) | copy-start | bytes 3538948
  1.9 0.9 %copy-start.1 = (bf16[3,96,256]{2,1,0:T(8,128)(2,1)S(1)}, bf16[3,96,256]{2,1,0:T(8,128)(2,1)}, u32[]{:S(2)}) copy-start(bf16[3,96,256]{2,1,0:T(8,128)(2,1)} %v_ref.1) | copy-start | bytes 442372
